TPU v7x, 256 devices: a whole 4x4x8 slice. The times are simulated.
256 devices in a mesh: section: 8 (over x, core), row: 8 (over z), col: 4 (over y).
Axes of the slice: x: 4, y: 4, z: 8, core: 2. Of those that a mesh axis runs over, the one named last changes fastest.
Arguments:
- frames: bfloat16 [2, 6, 16, 64, 128], P(None, None, None, 'row', 'col'), may hold values from -6 to 6
- region_order: int32 [6], replicated, may hold values from 0 to 5, each once
- encoder: bfloat16 [64, 16], replicated, may hold values from -1.5 to 1.5
- input_kernel: bfloat16 [8, 448, 1600], P('section'), may hold values from -0.15625 to 0.15625
- hidden_kernel: bfloat16 [8, 256, 1600], P('section'), may hold values from -0.15625 to 0.15625
- memory_kernel: bfloat16 [8, 192, 1600], P('section'), may hold values from -0.15625 to 0.15625
- output_kernel: bfloat16 [8, 64, 3200], P('section'), may hold values from -0.109375 to 0.109375
- mixing_weight: bfloat16 [8, 64, 128], P('section'), may hold values from -0.5 to 0.5
- hidden_start: float32 [8, 3, 64, 64, 128], P('section', None, None, 'row', 'col'), may hold values from -0.9 to 0.9
- cell_start: float32 [8, 3, 64, 64, 128], P('section', None, None, 'row', 'col'), may hold values from -5 to 5
- memory_start: float32 [3, 64, 64, 128], P(None, None, 'row', 'col'), may hold values from -5 to 5
Outputs:
- hidden_final: float32 [8, 3, 64, 64, 128], P('section', None, None, 'row', 'col')
- cell_final: float32 [8, 3, 64, 64, 128], P('section', None, None, 'row', 'col')
- memory_final: float32 [8, 3, 64, 64, 128], P('section', None, None, 'row', 'col')
Inputs may be any that keep to these rules, and one draw needn't show every extreme that they name: A permutation of the regions; micro-batch b takes region region_order[b] for b < 3, the rest are unused.
All inputs are finite; a program needn't handle non-finite values.
Results may differ from a plain program's by a relative error of at most 0.017.
Values may be sent and summed in bfloat16 or wider, within the bound.
A program may use at most 64 MiB of HBM per device.

v0:
```python
import jax
import jax.numpy as jnp
from jax import lax
from jax.sharding import PartitionSpec as P

KS = 5


def extended(cells, sides, width):
    for axis, dim in sides:
        count = lax.axis_size(axis)
        ends = count - 1
        head = lax.slice_in_dim(cells, 0, width, axis=dim)
        tail = lax.slice_in_dim(cells, cells.shape[dim] - width, cells.shape[dim], axis=dim)
        cells = jnp.concatenate(
            [
                lax.ppermute(tail, axis, [(i, (i + 1) % count) for i in range(ends)]),
                cells,
                lax.ppermute(head, axis, [((i + 1) % count, i) for i in range(ends)]),
            ],
            axis=dim,
        )
    return cells


def passed_along(value, axis, by):
    length = lax.axis_size(axis)
    pairs = [(i, i + by) for i in range(length) if 0 <= i + by < length]
    return lax.ppermute(value, axis, pairs)


def shifted(value, axis, steps):
    count = lax.axis_size(axis)
    pairs = [(source, (source + steps) % count) for source in range(count)]
    return lax.ppermute(value, axis, pairs)


def conv_tiles(kernel, padded, out_rows, out_cols):
    in_channels = padded.shape[0]
    spread = padded.shape[1] - out_rows + 1
    pieces = [
        padded[:, tap_row : tap_row + out_rows, tap_col : tap_col + out_cols]
        for tap_row in range(spread)
        for tap_col in range(spread)
    ]
    stacked = jnp.stack(pieces).reshape(spread * spread * in_channels, out_rows * out_cols)
    return jnp.dot(kernel, stacked, preferred_element_type=jnp.float32)


def update_states(from_input, from_hidden, from_memory, cell_prev, memory_in):
    sigmoid = jax.nn.sigmoid
    channels = cell_prev.shape[0]
    input_parts = from_input.reshape(7, channels, -1)
    hidden_parts = from_hidden.reshape(4, channels, -1)
    memory_parts = from_memory.reshape(3, channels, -1)
    cell_new = sigmoid(input_parts[1] + hidden_parts[1] + 1.0) * cell_prev + sigmoid(
        input_parts[0] + hidden_parts[0]
    ) * jnp.tanh(input_parts[2] + hidden_parts[2])
    memory_new = sigmoid(input_parts[4] + memory_parts[1] + 1.0) * memory_in + sigmoid(
        input_parts[3] + memory_parts[0]
    ) * jnp.tanh(input_parts[5] + memory_parts[2])
    gate_part = input_parts[6] + hidden_parts[3]
    return (cell_new, memory_new, gate_part)


def emit_hidden(joined_padded, gate_part, output_kernel, mixing_weight, out_rows, out_cols, margin):
    out_gate = jax.nn.sigmoid(
        gate_part + conv_tiles(output_kernel, joined_padded, out_rows, out_cols)
    )
    interior = joined_padded[:, margin : margin + out_rows, margin : margin + out_cols].reshape(
        joined_padded.shape[0], out_rows * out_cols
    )
    mixed = jnp.dot(mixing_weight, interior, preferred_element_type=jnp.float32)
    return out_gate * jnp.tanh(mixed)


def per_device(
    frames,
    region_order,
    encoder,
    input_kernel,
    hidden_kernel,
    memory_kernel,
    output_kernel,
    mixing_weight,
    hidden_start,
    cell_start,
    memory_start,
):
    sections = lax.axis_size("section")
    position = lax.axis_index("section")
    steps_count = frames.shape[0]
    patch_channels = frames.shape[2]
    tile_rows = frames.shape[3]
    tile_cols = frames.shape[4]
    batches = memory_start.shape[0]
    channels = memory_start.shape[1]
    tile_count = tile_rows * tile_cols
    margin = KS // 2
    period = max(batches, sections)
    tick_count = (steps_count - 1) * period + batches + sections - 1
    gate_input = input_kernel[0]
    gate_hidden = hidden_kernel[0]
    gate_memory = memory_kernel[0]
    gate_output = output_kernel[0]
    gate_mixing = mixing_weight[0]
    tile_shape = (channels, tile_rows, tile_cols)

    def decode_item(item_offset):
        clipped = jnp.maximum(item_offset, 0)
        moment = clipped // period
        batch_index = clipped % period
        active = (item_offset >= 0) & (moment < steps_count) & (batch_index < batches)
        return (active, jnp.minimum(moment, steps_count - 1), jnp.minimum(batch_index, batches - 1))

    def first_half(padded, cell_prev, memory_in):
        from_input = conv_tiles(gate_input, padded[:channels], tile_rows, tile_cols)
        from_hidden = conv_tiles(gate_hidden, padded[channels : 2 * channels], tile_rows, tile_cols)
        from_memory = conv_tiles(gate_memory, padded[2 * channels :], tile_rows, tile_cols)
        cell_new, memory_new, gate_part = update_states(
            from_input,
            from_hidden,
            from_memory,
            cell_prev.reshape(channels, tile_count),
            memory_in.reshape(channels, tile_count),
        )
        return (cell_new.reshape(tile_shape), memory_new.reshape(tile_shape), gate_part)

    def first_spare(padded, cell_prev, memory_in):
        return (
            jnp.zeros(tile_shape, jnp.float32),
            jnp.zeros(tile_shape, jnp.float32),
            jnp.zeros((channels, tile_count), jnp.float32),
        )

    def second_half(joined_padded, gate_part):
        return emit_hidden(
            joined_padded, gate_part, gate_output, gate_mixing, tile_rows, tile_cols, margin
        ).reshape(tile_shape)

    def second_spare(joined_padded, gate_part):
        return jnp.zeros(tile_shape, jnp.float32)

    def advance(tick_index, carried):
        hidden_states, cell_states, memory_last, memory_loop, received_hidden, received_memory = (
            carried
        )
        active, moment, batch_index = decode_item(tick_index - position)
        frame_now = frames[moment, region_order[batch_index]]
        encoded = (
            jnp.dot(
                encoder,
                frame_now.reshape(patch_channels, tile_count),
                preferred_element_type=jnp.float32,
            )
            .astype(jnp.bfloat16)
            .reshape(tile_shape)
        )
        layer_input = jnp.where(position == 0, encoded, received_hidden)
        first_memory = jnp.where(moment == 0, memory_start[batch_index], memory_loop[batch_index])
        memory_in = jnp.where(position == 0, first_memory, received_memory)
        hidden_prev = hidden_states[batch_index]
        cell_prev = cell_states[batch_index]
        stacked = jnp.concatenate(
            [layer_input, hidden_prev.astype(jnp.bfloat16), memory_in.astype(jnp.bfloat16)], 0
        )
        padded = extended(stacked, (("row", 1), ("col", 2)), margin)
        cell_new, memory_new, gate_part = lax.cond(
            active, first_half, first_spare, padded, cell_prev, memory_in
        )
        joined = jnp.concatenate([cell_new, memory_new], 0).astype(jnp.bfloat16)
        joined_padded = extended(joined, (("row", 1), ("col", 2)), margin)
        hidden_new = lax.cond(active, second_half, second_spare, joined_padded, gate_part)
        hidden_states = lax.dynamic_update_index_in_dim(
            hidden_states, jnp.where(active, hidden_new, hidden_prev), batch_index, 0
        )
        cell_states = lax.dynamic_update_index_in_dim(
            cell_states, jnp.where(active, cell_new, cell_prev), batch_index, 0
        )
        memory_last = lax.dynamic_update_index_in_dim(
            memory_last, jnp.where(active, memory_new, memory_last[batch_index]), batch_index, 0
        )
        received_hidden = passed_along(hidden_new.astype(jnp.bfloat16), "section", 1)
        received_memory = shifted(memory_new.astype(jnp.bfloat16), "section", 1).astype(
            memory_new.dtype
        )
        top_active, top_moment, top_batch = decode_item(tick_index - (sections - 1))
        keep_top = top_active & (position == 0)
        memory_loop = lax.dynamic_update_index_in_dim(
            memory_loop, jnp.where(keep_top, received_memory, memory_loop[top_batch]), top_batch, 0
        )
        return (
            hidden_states,
            cell_states,
            memory_last,
            memory_loop,
            received_hidden,
            received_memory,
        )

    initial = (
        hidden_start[0],
        cell_start[0],
        jnp.zeros((batches,) + tile_shape, jnp.float32),
        jnp.zeros((batches,) + tile_shape, jnp.float32),
        jnp.zeros(tile_shape, jnp.bfloat16),
        jnp.zeros(tile_shape, jnp.float32),
    )
    hidden_states, cell_states, memory_last, memory_loop, received_hidden, received_memory = (
        lax.fori_loop(0, tick_count, advance, initial)
    )
    return (hidden_states[None], cell_states[None], memory_last[None])


def solution(mesh):
    return jax.shard_map(
        per_device,
        mesh=mesh,
        in_specs=(
            P(None, None, None, "row", "col"),
            P(),
            P(),
            P("section", None, None),
            P("section", None, None),
            P("section", None, None),
            P("section", None, None),
            P("section", None, None),
            P("section", None, None, "row", "col"),
            P("section", None, None, "row", "col"),
            P(None, None, "row", "col"),
        ),
        out_specs=(
            P("section", None, None, "row", "col"),
            P("section", None, None, "row", "col"),
            P("section", None, None, "row", "col"),
        ),
        check_vma=False,
    )
```

profile of v0, /device:TPU:39, one launch (start us, length us, event | category | flops | bytes accessed | tf_op | source)
XLA Modules:
  0.0 1269.6 jit_solution(2912326818309127308)
XLA Ops:
  7.2 1262.3 %while.27 = (s32[]{:T(128)}, f32[3,64,8,32]{1,3,2,0:T(8,128)}, f32[3,64,8,32]{1,3,2,0:T(8,128)}, f32[3,64,8,32]{1,3,2,0:T(8,128)}, f32[3,64,8,32]{1,3,2,0:T(8,12...) while((s32[]{:T(128)}, f32[3,64,8,32]{1,3,2,0:T(8,128)}, ...), condition=%wide.region_5.6_spmd.clone, body=%wide.region_0.5_spmd.clone.sunk | while | flops 846987328 | bytes 58680980 | solution.py:210
  34.0 20.7 %collective-permute-start.8 = (bf16[64,8,32]{0,2,1:T(8,128)(2,1)S(1)}, bf16[64,8,32]{0,2,1:T(8,128)(2,1)S(1)}, u32[]{:S(2)}, u32[]{:S(2)}) collective-permute-start(bf16[64,8,32]{0,2,1:T(8,128)(2,1)S(1)} %get-tuple-element.869), channel_id=1, source_target_pairs={{0,32},{32,64},{64,96},{96,128},{128,160},{160,192},{192,224},{224... | collective-permute-start | bytes 98312 | tf_op jit(solution)/shard_map/while/body/eval_jaxpr/ppermute | solution.py:35
  101.5 22.9 %collective-permute-start.8 = (bf16[64,8,32]{0,2,1:T(8,128)(2,1)S(1)}, bf16[64,8,32]{0,2,1:T(8,128)(2,1)S(1)}, u32[]{:S(2)}, u32[]{:S(2)}) collective-permute-start(bf16[64,8,32]{0,2,1:T(8,128)(2,1)S(1)} %get-tuple-element.869), channel_id=1, source_target_pairs={{0,32},{32,64},{64,96},{96,128},{128,160},{160,192},{192,224},{224... | collective-permute-start | bytes 98312 | tf_op jit(solution)/shard_map/while/body/eval_jaxpr/ppermute | solution.py:35
  172.1 22.2 %collective-permute-start.8 = (bf16[64,8,32]{0,2,1:T(8,128)(2,1)S(1)}, bf16[64,8,32]{0,2,1:T(8,128)(2,1)S(1)}, u32[]{:S(2)}, u32[]{:S(2)}) collective-permute-start(bf16[64,8,32]{0,2,1:T(8,128)(2,1)S(1)} %get-tuple-element.869), channel_id=1, source_target_pairs={{0,32},{32,64},{64,96},{96,128},{128,160},{160,192},{192,224},{224... | collective-permute-start | bytes 98312 | tf_op jit(solution)/shard_map/while/body/eval_jaxpr/ppermute | solution.py:35
  294.5 25.9 %collective-permute-start.8 = (bf16[64,8,32]{0,2,1:T(8,128)(2,1)S(1)}, bf16[64,8,32]{0,2,1:T(8,128)(2,1)S(1)}, u32[]{:S(2)}, u32[]{:S(2)}) collective-permute-start(bf16[64,8,32]{0,2,1:T(8,128)(2,1)S(1)} %get-tuple-element.869), channel_id=1, source_target_pairs={{0,32},{32,64},{64,96},{96,128},{128,160},{160,192},{192,224},{224... | collective-permute-start | bytes 98312 | tf_op jit(solution)/shard_map/while/body/eval_jaxpr/ppermute | solution.py:35
  368.4 23.8 %collective-permute-start.8 = (bf16[64,8,32]{0,2,1:T(8,128)(2,1)S(1)}, bf16[64,8,32]{0,2,1:T(8,128)(2,1)S(1)}, u32[]{:S(2)}, u32[]{:S(2)}) collective-permute-start(bf16[64,8,32]{0,2,1:T(8,128)(2,1)S(1)} %get-tuple-element.869), channel_id=1, source_target_pairs={{0,32},{32,64},{64,96},{96,128},{128,160},{160,192},{192,224},{224... | collective-permute-start | bytes 98312 | tf_op jit(solution)/shard_map/while/body/eval_jaxpr/ppermute | solution.py:35
  440.2 6.9 collective-permute-start.8
  465.0 13.2 %collective-permute-done.8 = bf16[64,8,32]{0,2,1:T(8,128)(2,1)S(1)} collective-permute-done((bf16[64,8,32]{0,2,1:T(8,128)(2,1)S(1)}, bf16[64,8,32]{0,2,1:T(8,128)(2,1)S(1)}, u32[]{:S(2)}, u32[]{:S(2)}) %collective-permute-start.8) | collective-permute-done | bytes 32800 | tf_op jit(solution)/shard_map/while/body/eval_jaxpr/ppermute | solution.py:35
  478.8 21.1 %collective-permute-done.9 = bf16[64,8,32]{0,2,1:T(8,128)(2,1)S(1)} collective-permute-done((bf16[64,8,32]{0,2,1:T(8,128)(2,1)S(1)}, bf16[64,8,32]{0,2,1:T(8,128)(2,1)S(1)}, u32[]{:S(2)}, u32[]{:S(2)}) %collective-permute-start.9) | collective-permute-done | bytes 32800 | tf_op jit(solution)/shard_map/while/body/eval_jaxpr/ppermute | solution.py:29
  509.8 4.9 collective-permute-start.1
  527.1 20.4 %conditional.6 = (f32[64,8,32]{0,2,1:T(8,128)}, f32[64,8,32]{0,2,1:T(8,128)}, f32[64,256]{1,0:T(8,128)S(1)}, bf16[64,8,32]{0,2,1:T(8,128)(2,1)S(1)}, bf16[64,8,32]{0,2,1:T(8,128)(2,1)S(1)}) conditional(s32[]{:T(128)} %convert_element_type.109, () %tuple.155, (bf16[192,12,36]{0,2,1:T(8,128)(2,1)S(1)}, bf16[448,1600]{1,0:T(8,128)(2,1)}, ...), branch_computations={%region_1.1_spmd, %region_2.2_spmd} | conditional | flops 734478336 | bytes 42844396 | solution.py:168
  549.7 4.9 collective-permute-start.5
  568.5 5.4 collective-permute-done.9
  583.7 4.9 collective-permute-start.1
  601.1 20.4 %conditional.6 = (f32[64,8,32]{0,2,1:T(8,128)}, f32[64,8,32]{0,2,1:T(8,128)}, f32[64,256]{1,0:T(8,128)S(1)}, bf16[64,8,32]{0,2,1:T(8,128)(2,1)S(1)}, bf16[64,8,32]{0,2,1:T(8,128)(2,1)S(1)}) conditional(s32[]{:T(128)} %convert_element_type.109, () %tuple.155, (bf16[192,12,36]{0,2,1:T(8,128)(2,1)S(1)}, bf16[448,1600]{1,0:T(8,128)(2,1)}, ...), branch_computations={%region_1.1_spmd, %region_2.2_spmd} | conditional | flops 734478336 | bytes 42844396 | solution.py:168
  623.6 4.9 collective-permute-start.5
  642.4 5.3 collective-permute-done.9
  657.6 4.9 collective-permute-start.1
  675.0 20.4 %conditional.6 = (f32[64,8,32]{0,2,1:T(8,128)}, f32[64,8,32]{0,2,1:T(8,128)}, f32[64,256]{1,0:T(8,128)S(1)}, bf16[64,8,32]{0,2,1:T(8,128)(2,1)S(1)}, bf16[64,8,32]{0,2,1:T(8,128)(2,1)S(1)}) conditional(s32[]{:T(128)} %convert_element_type.109, () %tuple.155, (bf16[192,12,36]{0,2,1:T(8,128)(2,1)S(1)}, bf16[448,1600]{1,0:T(8,128)(2,1)}, ...), branch_computations={%region_1.1_spmd, %region_2.2_spmd} | conditional | flops 734478336 | bytes 42844396 | solution.py:168
  850.3 22.1 %collective-permute-start.8 = (bf16[64,8,32]{0,2,1:T(8,128)(2,1)S(1)}, bf16[64,8,32]{0,2,1:T(8,128)(2,1)S(1)}, u32[]{:S(2)}, u32[]{:S(2)}) collective-permute-start(bf16[64,8,32]{0,2,1:T(8,128)(2,1)S(1)} %get-tuple-element.869), channel_id=1, source_target_pairs={{0,32},{32,64},{64,96},{96,128},{128,160},{160,192},{192,224},{224... | collective-permute-start | bytes 98312 | tf_op jit(solution)/shard_map/while/body/eval_jaxpr/ppermute | solution.py:35
  920.4 23.8 %collective-permute-start.8 = (bf16[64,8,32]{0,2,1:T(8,128)(2,1)S(1)}, bf16[64,8,32]{0,2,1:T(8,128)(2,1)S(1)}, u32[]{:S(2)}, u32[]{:S(2)}) collective-permute-start(bf16[64,8,32]{0,2,1:T(8,128)(2,1)S(1)} %get-tuple-element.869), channel_id=1, source_target_pairs={{0,32},{32,64},{64,96},{96,128},{128,160},{160,192},{192,224},{224... | collective-permute-start | bytes 98312 | tf_op jit(solution)/shard_map/while/body/eval_jaxpr/ppermute | solution.py:35
  992.2 6.9 collective-permute-start.8
  1017.0 13.2 %collective-permute-done.8 = bf16[64,8,32]{0,2,1:T(8,128)(2,1)S(1)} collective-permute-done((bf16[64,8,32]{0,2,1:T(8,128)(2,1)S(1)}, bf16[64,8,32]{0,2,1:T(8,128)(2,1)S(1)}, u32[]{:S(2)}, u32[]{:S(2)}) %collective-permute-start.8) | collective-permute-done | bytes 32800 | tf_op jit(solution)/shard_map/while/body/eval_jaxpr/ppermute | solution.py:35
  1030.9 21.1 %collective-permute-done.9 = bf16[64,8,32]{0,2,1:T(8,128)(2,1)S(1)} collective-permute-done((bf16[64,8,32]{0,2,1:T(8,128)(2,1)S(1)}, bf16[64,8,32]{0,2,1:T(8,128)(2,1)S(1)}, u32[]{:S(2)}, u32[]{:S(2)}) %collective-permute-start.9) | collective-permute-done | bytes 32800 | tf_op jit(solution)/shard_map/while/body/eval_jaxpr/ppermute | solution.py:29
  1061.9 4.9 collective-permute-start.1
  1079.2 20.4 %conditional.6 = (f32[64,8,32]{0,2,1:T(8,128)}, f32[64,8,32]{0,2,1:T(8,128)}, f32[64,256]{1,0:T(8,128)S(1)}, bf16[64,8,32]{0,2,1:T(8,128)(2,1)S(1)}, bf16[64,8,32]{0,2,1:T(8,128)(2,1)S(1)}) conditional(s32[]{:T(128)} %convert_element_type.109, () %tuple.155, (bf16[192,12,36]{0,2,1:T(8,128)(2,1)S(1)}, bf16[448,1600]{1,0:T(8,128)(2,1)}, ...), branch_computations={%region_1.1_spmd, %region_2.2_spmd} | conditional | flops 734478336 | bytes 42844396 | solution.py:168
  1120.6 5.3 collective-permute-done.9
  1135.8 4.9 collective-permute-start.1
  1153.1 20.4 %conditional.6 = (f32[64,8,32]{0,2,1:T(8,128)}, f32[64,8,32]{0,2,1:T(8,128)}, f32[64,256]{1,0:T(8,128)S(1)}, bf16[64,8,32]{0,2,1:T(8,128)(2,1)S(1)}, bf16[64,8,32]{0,2,1:T(8,128)(2,1)S(1)}) conditional(s32[]{:T(128)} %convert_element_type.109, () %tuple.155, (bf16[192,12,36]{0,2,1:T(8,128)(2,1)S(1)}, bf16[448,1600]{1,0:T(8,128)(2,1)}, ...), branch_computations={%region_1.1_spmd, %region_2.2_spmd} | conditional | flops 734478336 | bytes 42844396 | solution.py:168
  1194.5 5.4 collective-permute-done.9
  1209.7 4.9 collective-permute-start.1
  1227.0 20.4 %conditional.6 = (f32[64,8,32]{0,2,1:T(8,128)}, f32[64,8,32]{0,2,1:T(8,128)}, f32[64,256]{1,0:T(8,128)S(1)}, bf16[64,8,32]{0,2,1:T(8,128)(2,1)S(1)}, bf16[64,8,32]{0,2,1:T(8,128)(2,1)S(1)}) conditional(s32[]{:T(128)} %convert_element_type.109, () %tuple.155, (bf16[192,12,36]{0,2,1:T(8,128)(2,1)S(1)}, bf16[448,1600]{1,0:T(8,128)(2,1)}, ...), branch_computations={%region_1.1_spmd, %region_2.2_spmd} | conditional | flops 734478336 | bytes 42844396 | solution.py:168
  (1486 shorter events, 955.2 us)
Async XLA Ops:
  34.0 38.2 %collective-permute-start.8 = (bf16[64,8,32]{0,2,1:T(8,128)(2,1)S(1)}, bf16[64,8,32]{0,2,1:T(8,128)(2,1)S(1)}, u32[]{:S(2)}, u32[]{:S(2)}) collective-permute-start(bf16[64,8,32]{0,2,1:T(8,128)(2,1)S(1)} %get-tuple-element.869), channel_id=1, source_target_pairs={{0,32},{32,64},{64,96},{96,128},{128,160},{160,192},{192,224},{224... | collective-permute-start | bytes 98312 | tf_op jit(solution)/shard_map/while/body/eval_jaxpr/ppermute | solution.py:35
  101.5 40.4 %collective-permute-start.8 = (bf16[64,8,32]{0,2,1:T(8,128)(2,1)S(1)}, bf16[64,8,32]{0,2,1:T(8,128)(2,1)S(1)}, u32[]{:S(2)}, u32[]{:S(2)}) collective-permute-start(bf16[64,8,32]{0,2,1:T(8,128)(2,1)S(1)} %get-tuple-element.869), channel_id=1, source_target_pairs={{0,32},{32,64},{64,96},{96,128},{128,160},{160,192},{192,224},{224... | collective-permute-start | bytes 98312 | tf_op jit(solution)/shard_map/while/body/eval_jaxpr/ppermute | solution.py:35
  172.1 40.4 %collective-permute-start.8 = (bf16[64,8,32]{0,2,1:T(8,128)(2,1)S(1)}, bf16[64,8,32]{0,2,1:T(8,128)(2,1)S(1)}, u32[]{:S(2)}, u32[]{:S(2)}) collective-permute-start(bf16[64,8,32]{0,2,1:T(8,128)(2,1)S(1)} %get-tuple-element.869), channel_id=1, source_target_pairs={{0,32},{32,64},{64,96},{96,128},{128,160},{160,192},{192,224},{224... | collective-permute-start | bytes 98312 | tf_op jit(solution)/shard_map/while/body/eval_jaxpr/ppermute | solution.py:35
  222.2 11.5 collective-permute-start
  242.6 21.7 %collective-permute-start.8 = (bf16[64,8,32]{0,2,1:T(8,128)(2,1)S(1)}, bf16[64,8,32]{0,2,1:T(8,128)(2,1)S(1)}, u32[]{:S(2)}, u32[]{:S(2)}) collective-permute-start(bf16[64,8,32]{0,2,1:T(8,128)(2,1)S(1)} %get-tuple-element.869), channel_id=1, source_target_pairs={{0,32},{32,64},{64,96},{96,128},{128,160},{160,192},{192,224},{224... | collective-permute-start | bytes 98312 | tf_op jit(solution)/shard_map/while/body/eval_jaxpr/ppermute | solution.py:35
  274.1 11.5 collective-permute-start
  294.5 43.8 %collective-permute-start.8 = (bf16[64,8,32]{0,2,1:T(8,128)(2,1)S(1)}, bf16[64,8,32]{0,2,1:T(8,128)(2,1)S(1)}, u32[]{:S(2)}, u32[]{:S(2)}) collective-permute-start(bf16[64,8,32]{0,2,1:T(8,128)(2,1)S(1)} %get-tuple-element.869), channel_id=1, source_target_pairs={{0,32},{32,64},{64,96},{96,128},{128,160},{160,192},{192,224},{224... | collective-permute-start | bytes 98312 | tf_op jit(solution)/shard_map/while/body/eval_jaxpr/ppermute | solution.py:35
  348.0 11.5 collective-permute-start
  368.4 41.7 %collective-permute-start.8 = (bf16[64,8,32]{0,2,1:T(8,128)(2,1)S(1)}, bf16[64,8,32]{0,2,1:T(8,128)(2,1)S(1)}, u32[]{:S(2)}, u32[]{:S(2)}) collective-permute-start(bf16[64,8,32]{0,2,1:T(8,128)(2,1)S(1)} %get-tuple-element.869), channel_id=1, source_target_pairs={{0,32},{32,64},{64,96},{96,128},{128,160},{160,192},{192,224},{224... | collective-permute-start | bytes 98312 | tf_op jit(solution)/shard_map/while/body/eval_jaxpr/ppermute | solution.py:35
  419.8 11.5 collective-permute-start
  440.2 37.9 %collective-permute-start.8 = (bf16[64,8,32]{0,2,1:T(8,128)(2,1)S(1)}, bf16[64,8,32]{0,2,1:T(8,128)(2,1)S(1)}, u32[]{:S(2)}, u32[]{:S(2)}) collective-permute-start(bf16[64,8,32]{0,2,1:T(8,128)(2,1)S(1)} %get-tuple-element.869), channel_id=1, source_target_pairs={{0,32},{32,64},{64,96},{96,128},{128,160},{160,192},{192,224},{224... | collective-permute-start | bytes 98312 | tf_op jit(solution)/shard_map/while/body/eval_jaxpr/ppermute | solution.py:35
  463.7 36.3 %collective-permute-start.9 = (bf16[64,8,32]{0,2,1:T(8,128)(2,1)S(1)}, bf16[64,8,32]{0,2,1:T(8,128)(2,1)S(1)}, u32[]{:S(2)}, u32[]{:S(2)}) collective-permute-start(bf16[64,8,32]{0,2,1:T(8,128)(2,1)S(1)} %convert_element_type.110), channel_id=1, source_target_pairs={{0,32},{32,64},{64,96},{96,128},{128,160},{160,192},{192,224},{1,3... | collective-permute-start | bytes 98312 | tf_op jit(solution)/shard_map/while/body/eval_jaxpr/ppermute | solution.py:29
  507.9 11.5 collective-permute-start
  547.5 20.3 %collective-permute-start.8 = (bf16[64,8,32]{0,2,1:T(8,128)(2,1)S(1)}, bf16[64,8,32]{0,2,1:T(8,128)(2,1)S(1)}, u32[]{:S(2)}, u32[]{:S(2)}) collective-permute-start(bf16[64,8,32]{0,2,1:T(8,128)(2,1)S(1)} %get-tuple-element.869), channel_id=1, source_target_pairs={{0,32},{32,64},{64,96},{96,128},{128,160},{160,192},{192,224},{224... | collective-permute-start | bytes 98312 | tf_op jit(solution)/shard_map/while/body/eval_jaxpr/ppermute | solution.py:35
  581.8 11.5 collective-permute-start
  621.4 20.3 %collective-permute-start.8 = (bf16[64,8,32]{0,2,1:T(8,128)(2,1)S(1)}, bf16[64,8,32]{0,2,1:T(8,128)(2,1)S(1)}, u32[]{:S(2)}, u32[]{:S(2)}) collective-permute-start(bf16[64,8,32]{0,2,1:T(8,128)(2,1)S(1)} %get-tuple-element.869), channel_id=1, source_target_pairs={{0,32},{32,64},{64,96},{96,128},{128,160},{160,192},{192,224},{224... | collective-permute-start | bytes 98312 | tf_op jit(solution)/shard_map/while/body/eval_jaxpr/ppermute | solution.py:35
  655.7 11.6 collective-permute-start
  695.4 20.3 %collective-permute-start.8 = (bf16[64,8,32]{0,2,1:T(8,128)(2,1)S(1)}, bf16[64,8,32]{0,2,1:T(8,128)(2,1)S(1)}, u32[]{:S(2)}, u32[]{:S(2)}) collective-permute-start(bf16[64,8,32]{0,2,1:T(8,128)(2,1)S(1)} %get-tuple-element.869), channel_id=1, source_target_pairs={{0,32},{32,64},{64,96},{96,128},{128,160},{160,192},{192,224},{224... | collective-permute-start | bytes 98312 | tf_op jit(solution)/shard_map/while/body/eval_jaxpr/ppermute | solution.py:35
  745.6 21.2 %collective-permute-start.8 = (bf16[64,8,32]{0,2,1:T(8,128)(2,1)S(1)}, bf16[64,8,32]{0,2,1:T(8,128)(2,1)S(1)}, u32[]{:S(2)}, u32[]{:S(2)}) collective-permute-start(bf16[64,8,32]{0,2,1:T(8,128)(2,1)S(1)} %get-tuple-element.869), channel_id=1, source_target_pairs={{0,32},{32,64},{64,96},{96,128},{128,160},{160,192},{192,224},{224... | collective-permute-start | bytes 98312 | tf_op jit(solution)/shard_map/while/body/eval_jaxpr/ppermute | solution.py:35
  776.9 11.5 collective-permute-start
  797.6 20.8 %collective-permute-start.8 = (bf16[64,8,32]{0,2,1:T(8,128)(2,1)S(1)}, bf16[64,8,32]{0,2,1:T(8,128)(2,1)S(1)}, u32[]{:S(2)}, u32[]{:S(2)}) collective-permute-start(bf16[64,8,32]{0,2,1:T(8,128)(2,1)S(1)} %get-tuple-element.869), channel_id=1, source_target_pairs={{0,32},{32,64},{64,96},{96,128},{128,160},{160,192},{192,224},{224... | collective-permute-start | bytes 98312 | tf_op jit(solution)/shard_map/while/body/eval_jaxpr/ppermute | solution.py:35
  850.3 40.0 %collective-permute-start.8 = (bf16[64,8,32]{0,2,1:T(8,128)(2,1)S(1)}, bf16[64,8,32]{0,2,1:T(8,128)(2,1)S(1)}, u32[]{:S(2)}, u32[]{:S(2)}) collective-permute-start(bf16[64,8,32]{0,2,1:T(8,128)(2,1)S(1)} %get-tuple-element.869), channel_id=1, source_target_pairs={{0,32},{32,64},{64,96},{96,128},{128,160},{160,192},{192,224},{224... | collective-permute-start | bytes 98312 | tf_op jit(solution)/shard_map/while/body/eval_jaxpr/ppermute | solution.py:35
  900.0 11.5 collective-permute-start
  920.4 41.7 %collective-permute-start.8 = (bf16[64,8,32]{0,2,1:T(8,128)(2,1)S(1)}, bf16[64,8,32]{0,2,1:T(8,128)(2,1)S(1)}, u32[]{:S(2)}, u32[]{:S(2)}) collective-permute-start(bf16[64,8,32]{0,2,1:T(8,128)(2,1)S(1)} %get-tuple-element.869), channel_id=1, source_target_pairs={{0,32},{32,64},{64,96},{96,128},{128,160},{160,192},{192,224},{224... | collective-permute-start | bytes 98312 | tf_op jit(solution)/shard_map/while/body/eval_jaxpr/ppermute | solution.py:35
  992.2 38.0 %collective-permute-start.8 = (bf16[64,8,32]{0,2,1:T(8,128)(2,1)S(1)}, bf16[64,8,32]{0,2,1:T(8,128)(2,1)S(1)}, u32[]{:S(2)}, u32[]{:S(2)}) collective-permute-start(bf16[64,8,32]{0,2,1:T(8,128)(2,1)S(1)} %get-tuple-element.869), channel_id=1, source_target_pairs={{0,32},{32,64},{64,96},{96,128},{128,160},{160,192},{192,224},{224... | collective-permute-start | bytes 98312 | tf_op jit(solution)/shard_map/while/body/eval_jaxpr/ppermute | solution.py:35
  1015.7 36.3 %collective-permute-start.9 = (bf16[64,8,32]{0,2,1:T(8,128)(2,1)S(1)}, bf16[64,8,32]{0,2,1:T(8,128)(2,1)S(1)}, u32[]{:S(2)}, u32[]{:S(2)}) collective-permute-start(bf16[64,8,32]{0,2,1:T(8,128)(2,1)S(1)} %convert_element_type.110), channel_id=1, source_target_pairs={{0,32},{32,64},{64,96},{96,128},{128,160},{160,192},{192,224},{1,3... | collective-permute-start | bytes 98312 | tf_op jit(solution)/shard_map/while/body/eval_jaxpr/ppermute | solution.py:29
  1059.9 11.5 collective-permute-start
  1099.6 20.3 %collective-permute-start.8 = (bf16[64,8,32]{0,2,1:T(8,128)(2,1)S(1)}, bf16[64,8,32]{0,2,1:T(8,128)(2,1)S(1)}, u32[]{:S(2)}, u32[]{:S(2)}) collective-permute-start(bf16[64,8,32]{0,2,1:T(8,128)(2,1)S(1)} %get-tuple-element.869), channel_id=1, source_target_pairs={{0,32},{32,64},{64,96},{96,128},{128,160},{160,192},{192,224},{224... | collective-permute-start | bytes 98312 | tf_op jit(solution)/shard_map/while/body/eval_jaxpr/ppermute | solution.py:35
  1133.8 11.6 collective-permute-start
  1173.5 20.3 %collective-permute-start.8 = (bf16[64,8,32]{0,2,1:T(8,128)(2,1)S(1)}, bf16[64,8,32]{0,2,1:T(8,128)(2,1)S(1)}, u32[]{:S(2)}, u32[]{:S(2)}) collective-permute-start(bf16[64,8,32]{0,2,1:T(8,128)(2,1)S(1)} %get-tuple-element.869), channel_id=1, source_target_pairs={{0,32},{32,64},{64,96},{96,128},{128,160},{160,192},{192,224},{224... | collective-permute-start | bytes 98312 | tf_op jit(solution)/shard_map/while/body/eval_jaxpr/ppermute | solution.py:35
  1207.8 11.5 collective-permute-start
  1247.4 20.3 %collective-permute-start.8 = (bf16[64,8,32]{0,2,1:T(8,128)(2,1)S(1)}, bf16[64,8,32]{0,2,1:T(8,128)(2,1)S(1)}, u32[]{:S(2)}, u32[]{:S(2)}) collective-permute-start(bf16[64,8,32]{0,2,1:T(8,128)(2,1)S(1)} %get-tuple-element.869), channel_id=1, source_target_pairs={{0,32},{32,64},{64,96},{96,128},{128,160},{160,192},{192,224},{224... | collective-permute-start | bytes 98312 | tf_op jit(solution)/shard_map/while/body/eval_jaxpr/ppermute | solution.py:35
  (246 other events, 1664.0 us)
where the time goes:
time: 1280 us; the launch traced here: 1270 us
  starting transfers between devices  649 us (51%)
  local copies, waits for them, and re-layouts  295 us (23%)
  waiting for transfers between devices  118 us (9%)
  other arithmetic  105 us (8%)
  matrix products  57.7 us (5%)
  loops' own time  43.6 us (3%)
    ppermute x72, starting transfers between devices, extended(): lax.ppermute(tail, axis, [(i, (i + 1) % count) for i in range(ends)])  323 us
    ppermute x18, starting transfers between devices, shifted(): return lax.ppermute(value, axis, pairs)  185 us
    ppermute x72, starting transfers between devices, extended(): lax.ppermute(head, axis, [((i + 1) % count, i) for i in range(ends)])  119 us
    ppermute x18, waiting for transfers between devices, passed_along(): return lax.ppermute(value, axis, pairs)  79.1 us
    dot_general x24, matrix products, conv_tiles(): return jnp.dot(kernel, stacked, preferred_element_type=jnp.float32)  40.9 us
    another operation x1, loops' own time, per_device(): lax.fori_loop(0, tick_count, advance, initial)  40.9 us
    dynamic_slice x36, local copies, waits for them, and re-layouts, advance(): frame_now = frames[moment, region_order[batch_index]]  37.3 us
    cond x372, local copies, waits for them, and re-layouts  33.3 us
  transfers between devices with their start and end apart: 180, of which 39 were waited for; matrix products, arithmetic and copies ran while one was open for 15% of the time, Pallas kernels for 0%

commit v1 on v0

v1 whole, which is shorter than its diff:
```python
import functools

import jax
import jax.numpy as jnp
from jax import lax
from jax.experimental import pallas as pl
from jax.experimental.pallas import tpu as pltpu
from jax.sharding import PartitionSpec as P

KS = 5
HALO = 4
SIDE = 16
EDGE = 8
DIRS = [(dr, dc) for dr in (-1, 0, 1) for dc in (-1, 0, 1)]
MESH = pl.DeviceIdType.MESH


def sigmoid(value):
    return 0.5 * jnp.tanh(0.5 * value) + 0.5


def kernel_body(
    sections,
    rows,
    cols,
    steps,
    batches,
    enc_ref,
    hid_ref,
    cel_ref,
    mem_ref,
    wx_ref,
    wh_ref,
    wm_ref,
    wo_ref,
    wmix_ref,
    outh_ref,
    outs_ref,
    xwin,
    mwin,
    hwin,
    cwin,
    wide,
    p01,
    p23,
    p4,
    acc,
    state,
    joined,
    js,
    hbuf,
    mbuf,
    e_send,
    f_send,
    i_send,
    x_send,
    x_recv,
    m_send,
    m_recv,
    h_send,
    h_recv,
    c_send,
    c_recv,
    o_sem,
):
    sec = lax.axis_index("section")
    row = lax.axis_index("row")
    col = lax.axis_index("col")
    tr, tc = enc_ref.shape[1], enc_ref.shape[2]
    gr, gc = tr + 4, tc + 2 * EDGE
    wr = tr + 2 * HALO
    items = steps * batches
    first = sec == 0
    last = sec == sections - 1
    after = lax.rem(sec + 1, sections)
    before = lax.rem(sec + sections - 1, sections)

    def exists(dr, dc):
        found = None
        for ok in (
            row > 0 if dr < 0 else row < rows - 1 if dr > 0 else None,
            col > 0 if dc < 0 else col < cols - 1 if dc > 0 else None,
        ):
            if ok is not None:
                found = ok if found is None else found & ok
        return found

    def guarded(cond, fn):
        if cond is None:
            fn()
        else:
            pl.when(cond)(fn)

    def both(a, b):
        return b if a is None else a if b is None else a & b

    def src_part(dr, dc):
        rs = pl.ds(0, HALO) if dr < 0 else pl.ds(tr - HALO, HALO) if dr > 0 else pl.ds(0, tr)
        cs = pl.ds(0, SIDE) if dc < 0 else pl.ds(tc - SIDE, SIDE) if dc > 0 else pl.ds(0, tc)
        return rs, cs

    def dst_part(dr, dc):
        rs = pl.ds(HALO + tr, HALO) if dr < 0 else pl.ds(0, HALO) if dr > 0 else pl.ds(HALO, tr)
        cs = pl.ds(SIDE + tc, SIDE) if dc < 0 else pl.ds(0, SIDE) if dc > 0 else pl.ds(SIDE, tc)
        return rs, cs

    def copy_of(src, src_item, dst, dst_item, send_sem, recv_sem, target, index):
        dr, dc = DIRS[index]
        srs, scs = src_part(dr, dc)
        drs, dcs = dst_part(dr, dc)
        return pltpu.make_async_remote_copy(
            src_ref=src.at[src_item, srs, scs],
            dst_ref=dst.at[dst_item, drs, dcs],
            send_sem=send_sem.at[src_item, index],
            recv_sem=recv_sem.at[dst_item, index],
            device_id={
                "section": target,
                "row": lax.rem(row + dr + rows, rows),
                "col": lax.rem(col + dc + cols, cols),
            },
            device_id_type=MESH,
        )

    def each(indices, cond, fn):
        for index in indices:
            guarded(both(cond, exists(*DIRS[index])), functools.partial(fn, index))

    def each_source(indices, cond, fn):
        for index in indices:
            dr, dc = DIRS[index]
            guarded(both(cond, exists(-dr, -dc)), functools.partial(fn, index))

    every = list(range(9))
    around = [i for i in every if DIRS[i] != (0, 0)]
    centre = [DIRS.index((0, 0))]

    centre_rows, centre_cols = pl.ds(HALO, tr), pl.ds(SIDE, tc)

    def clear(k, _):
        zero = jnp.zeros(xwin.shape[1:], jnp.bfloat16)
        xwin[k] = zero
        mwin[k] = zero
        hwin[k] = zero
        return 0

    lax.fori_loop(0, items, clear, 0)

    def clear_cells(b, _):
        cwin[b] = jnp.zeros(cwin.shape[1:], jnp.float32)
        return 0

    lax.fori_loop(0, batches, clear_cells, 0)
    js[:, gr] = jnp.zeros((KS, tc, 128), jnp.bfloat16)

    barrier = pltpu.get_barrier_semaphore()
    for index in every:
        dr, dc = DIRS[index]

        def greet(dr=dr, dc=dc):
            for target in (after, before) + (() if (dr, dc) == (0, 0) else (sec,)):
                pl.semaphore_signal(
                    barrier,
                    inc=1,
                    device_id={"section": target, "row": row + dr, "col": col + dc},
                    device_id_type=MESH,
                )

        guarded(exists(dr, dc), greet)
    near_rows = 1 + (row > 0).astype(jnp.int32) + (row < rows - 1).astype(jnp.int32)
    near_cols = 1 + (col > 0).astype(jnp.int32) + (col < cols - 1).astype(jnp.int32)
    pl.semaphore_wait(barrier, 3 * near_rows * near_cols - 1)

    def x_first(k, index):
        return copy_of(enc_ref, k, xwin, k, e_send, x_recv, sec, index)

    def m_first(b, index):
        return copy_of(mem_ref, b, mwin, b, f_send, m_recv, sec, index)

    def h_first(b, index):
        return copy_of(hid_ref, b, hwin, b, i_send, h_recv, sec, index)

    def c_first(b, index):
        return copy_of(cel_ref, b, cwin, b, c_send, c_recv, sec, index)

    def x_next(k, index):
        return copy_of(hbuf, k, xwin, k, x_send, x_recv, after, index)

    def m_next(k, index):
        return copy_of(mbuf, k, mwin, k, m_send, m_recv, after, index)

    def m_loop(k, index):
        return copy_of(mbuf, k, mwin, k + batches, m_send, m_recv, after, index)

    def h_next(k, index):
        return copy_of(hbuf, k, hwin, k + batches, h_send, h_recv, sec, index)

    def h_own(k):
        return pltpu.make_async_copy(
            hbuf.at[k], hwin.at[k + batches, centre_rows, centre_cols], o_sem.at[k]
        )

    def start(make, k):
        return lambda index: make(k, index).start()

    def sent(make, k):
        return lambda index: make(k, index).wait_send()

    def landed(make, k):
        return lambda index: make(k, index).wait_recv()

    def begin(b, _):
        each(around, first, start(x_first, b))
        each(around, first, start(m_first, b))
        each(around, None, start(h_first, b))
        each(around, None, start(c_first, b))
        return 0

    lax.fori_loop(0, batches, begin, 0)

    def begin_later(k, _):
        each(around, first, start(x_first, k))
        return 0

    lax.fori_loop(batches, items, begin_later, 0)

    def place(b, _):
        hwin[b, centre_rows, centre_cols] = hid_ref[b]
        cwin[b, centre_rows, centre_cols] = cel_ref[b]
        return 0

    lax.fori_loop(0, batches, place, 0)

    @pl.when(first)
    def _():
        def place_first(b, _):
            mwin[b, centre_rows, centre_cols] = mem_ref[b]
            return 0

        lax.fori_loop(0, batches, place_first, 0)

        def place_input(k, _):
            xwin[k, centre_rows, centre_cols] = enc_ref[k]
            return 0

        lax.fori_loop(0, items, place_input, 0)

    low_lane = lax.broadcasted_iota(jnp.int32, (1, 1, 128), 2) < 64
    start_col = SIDE - EDGE - 2

    def spread(window):
        for r in range(wr):
            wide[r] = window[r].astype(jnp.float32)
        for r in range(wr):
            taps = [wide[r, pl.ds(start_col + q, gc), :] for q in range(KS)]
            p01[r] = jnp.where(low_lane[0], taps[0], taps[1]).astype(jnp.bfloat16)
            p23[r] = jnp.where(low_lane[0], taps[2], taps[3]).astype(jnp.bfloat16)
            below = wide[min(r + 1, wr - 1), pl.ds(start_col + 4, gc), :]
            p4[r] = jnp.where(low_lane[0], taps[4], below).astype(jnp.bfloat16)

    def patches():
        parts = []
        for p in range(KS):
            parts.append(p01[p : p + gr].reshape(gr * gc, 128))
            parts.append(p23[p : p + gr].reshape(gr * gc, 128))
        for p in (0, 2, 4):
            parts.append(p4[p : p + gr].reshape(gr * gc, 128))
        return jnp.concatenate(parts, axis=1)

    def cell(k, _):
        b = lax.rem(k, batches)
        early = k < batches
        late = k >= batches

        each_source(around, early, landed(h_first, b))
        each_source(around, late, landed(h_next, b))
        pl.when(late)(lambda: h_own(b).wait())
        spread(hwin.at[k])
        acc[...] = jnp.dot(patches(), wh_ref[...], preferred_element_type=jnp.float32)

        @pl.when(early)
        def _():
            each_source(around, None, landed(c_first, b))
            for r in range(gr):
                state[b, r] = cwin[b, r + HALO - 2, pl.ds(SIDE - EDGE, gc), :]

        each_source(around, first & early, landed(m_first, b))
        each_source(every, jnp.logical_not(first) | late, landed(m_next, k))
        spread(mwin.at[k])
        acc[...] += jnp.dot(patches(), wm_ref[...], preferred_element_type=jnp.float32)
        for r in range(gr):
            memory = wide[r + HALO - 2, pl.ds(SIDE - EDGE, gc), :]
            state[b, r] = jnp.where(low_lane[0], state[b, r], memory)

        each_source(around, first, landed(x_first, k))
        each_source(every, jnp.logical_not(first), landed(x_next, k))
        spread(xwin.at[k])
        acc[...] += jnp.dot(patches(), wx_ref[...], preferred_element_type=jnp.float32)

        grid_col = lax.broadcasted_iota(jnp.int32, (gc, 1), 0) + (col * tc - EDGE)
        col_ok = (grid_col >= 0) & (grid_col < cols * tc)
        for r in range(gr):
            part = acc[r * gc : (r + 1) * gc, :]
            new = sigmoid(part[:, 128:256] + 1.0) * state[b, r] + sigmoid(part[:, :128]) * jnp.tanh(
                part[:, 256:384]
            )
            state[b, r] = new
            grid_row = row * tr + (r - 2)
            ok = col_ok & ((grid_row >= 0) & (grid_row < rows * tr))
            joined[r] = jnp.where(ok, new, 0.0)

        tile = state[b, 2 : 2 + tr, EDGE : EDGE + tc, :]
        turned = pltpu.roll(tile.reshape(tr * tc, 128), 64, 1).reshape(tr, tc, 128)
        mbuf[k] = jnp.where(low_lane, turned, tile).astype(jnp.bfloat16)
        each(every, jnp.logical_not(last), start(m_next, k))
        each(every, last & early, start(m_loop, k))

        for q in range(KS):
            for r in range(gr):
                js[q, r] = joined[r, pl.ds(EDGE - 2 + q, tc), :].astype(jnp.bfloat16)
        parts = [
            js[q, 2 * g : 2 * g + tr + 1].reshape((tr + 1) * tc, 128)
            for g in range(3)
            for q in range(KS)
        ]
        out = jnp.dot(
            jnp.concatenate(parts, axis=1), wo_ref[...], preferred_element_type=jnp.float32
        )
        mixed = jnp.dot(
            js[2, 2 : 2 + tr].reshape(tr * tc, 128),
            wmix_ref[...],
            preferred_element_type=jnp.float32,
        )
        gate = out[: tr * tc, :128] + out[tc:, 128:]
        gate = gate.reshape(tr, tc, 128) + acc[2 * gc : (2 + tr) * gc, 384:].reshape(tr, gc, 128)[
            :, EDGE : EDGE + tc
        ]
        hidden = sigmoid(gate) * jnp.tanh(mixed).reshape(tr, tc, 128)
        hbuf[k] = hidden.astype(jnp.bfloat16)
        each(every, jnp.logical_not(last), start(x_next, k))

        @pl.when(early)
        def _():
            each(around, None, start(h_next, k))
            h_own(k).start()

        @pl.when(late)
        def _():
            outh_ref[b] = hidden
            outs_ref[b] = state[b, 2 : 2 + tr, EDGE : EDGE + tc, :]

        return 0

    lax.fori_loop(0, items, cell, 0)

    def finish(k, _):
        each(around, first, sent(x_first, k))
        each(every, jnp.logical_not(last), sent(x_next, k))
        each(every, jnp.logical_not(last), sent(m_next, k))
        return 0

    def finish_early(b, _):
        each(around, first, sent(m_first, b))
        each(every, last, sent(m_loop, b))
        each(around, None, sent(h_first, b))
        each(around, None, sent(h_next, b))
        each(around, None, sent(c_first, b))
        return 0

    lax.fori_loop(0, items, finish, 0)
    lax.fori_loop(0, batches, finish_early, 0)


def taps_first(blocks):
    turned = jnp.concatenate(blocks, 0).transpose(1, 2, 3, 0)
    wide = turned.shape[3]
    return jnp.concatenate(
        [
            turned[:, :4].reshape(-1, wide),
            turned[:, 4].reshape(-1, wide),
            jnp.zeros((turned.shape[2], wide), turned.dtype),
        ],
        0,
    )


def per_device(
    sizes,
    frames,
    region_order,
    encoder,
    input_kernel,
    hidden_kernel,
    memory_kernel,
    output_kernel,
    mixing_weight,
    hidden_start,
    cell_start,
    memory_start,
):
    bf16, f32 = jnp.bfloat16, jnp.float32
    sections, rows, cols = sizes
    steps, _, patch, tr, tc = frames.shape
    batches, ch = memory_start.shape[:2]
    items = steps * batches
    gr, gc = tr + 4, tc + 2 * EDGE
    wr, wc = tr + 2 * HALO, tc + 2 * SIDE

    ik = input_kernel[0].reshape(7, ch, KS, KS, ch)
    hk = hidden_kernel[0].reshape(4, ch, KS, KS, ch)
    mk = memory_kernel[0].reshape(3, ch, KS, KS, ch)
    none = jnp.zeros_like(ik[0])
    wx = taps_first([ik[0], ik[3], ik[1], ik[4], ik[2], ik[5], ik[6], ik[6]])
    wh = taps_first([hk[0], none, hk[1], none, hk[2], none, hk[3], hk[3]])
    wm = taps_first([none, mk[0], none, mk[1], none, mk[2], none, none])
    ok = output_kernel[0].reshape(ch, KS, KS, 2 * ch).transpose(1, 2, 3, 0)
    ok = jnp.concatenate([ok, jnp.zeros_like(ok[:1])], 0).reshape(3, 2, KS, 2 * ch, ch)
    wo = jnp.concatenate([ok[:, 0], ok[:, 0], ok[:, 1], ok[:, 1]], -1).reshape(-1, 4 * ch)
    wmix = jnp.concatenate([mixing_weight[0], mixing_weight[0]], 0).T

    def twice(value):
        return jnp.concatenate([value, value], -1)

    picked = jnp.take(frames, region_order[:batches], axis=1)
    enc = jnp.einsum("tbcyx,oc->tbyxo", picked, encoder, preferred_element_type=f32)
    enc = twice(enc.astype(bf16)).reshape(items, tr, tc, 2 * ch)
    hid = twice(hidden_start[0].transpose(0, 2, 3, 1).astype(bf16))
    cel = twice(cell_start[0].transpose(0, 2, 3, 1))
    mem = twice(memory_start.transpose(0, 2, 3, 1).astype(bf16))

    vmem = pl.BlockSpec(memory_space=pltpu.VMEM)
    dma = pltpu.SemaphoreType.DMA
    ends = jax.ShapeDtypeStruct((batches, tr, tc, 2 * ch), f32)
    outh, outs = pl.pallas_call(
        functools.partial(kernel_body, sections, rows, cols, steps, batches),
        out_shape=(ends, ends),
        in_specs=[vmem] * 9,
        out_specs=(vmem, vmem),
        scratch_shapes=[
            pltpu.VMEM((items, wr, wc, 128), bf16),
            pltpu.VMEM((items, wr, wc, 128), bf16),
            pltpu.VMEM((items, wr, wc, 128), bf16),
            pltpu.VMEM((batches, wr, wc, 128), f32),
            pltpu.VMEM((wr, wc, 128), f32),
            pltpu.VMEM((wr, gc, 128), bf16),
            pltpu.VMEM((wr, gc, 128), bf16),
            pltpu.VMEM((wr, gc, 128), bf16),
            pltpu.VMEM((gr * gc, 512), f32),
            pltpu.VMEM((batches, gr, gc, 128), f32),
            pltpu.VMEM((gr, gc, 128), f32),
            pltpu.VMEM((KS, gr + 1, tc, 128), bf16),
            pltpu.VMEM((items, tr, tc, 128), bf16),
            pltpu.VMEM((items, tr, tc, 128), bf16),
            dma((items, 9)),
            dma((batches, 9)),
            dma((batches, 9)),
            dma((items, 9)),
            dma((items, 9)),
            dma((items, 9)),
            dma((items, 9)),
            dma((batches, 9)),
            dma((items, 9)),
            dma((batches, 9)),
            dma((batches, 9)),
            dma((batches,)),
        ],
        compiler_params=pltpu.CompilerParams(
            collective_id=0, has_side_effects=True, vmem_limit_bytes=56 << 20
        ),
        name="predrnn",
    )(enc, hid, cel, mem, wx, wh, wm, wo, wmix)

    def back(value):
        return value.transpose(0, 3, 1, 2)[None]

    return back(outh[..., :ch]), back(outs[..., :ch]), back(outs[..., ch:])


def solution(mesh):
    sizes = tuple(mesh.shape[name] for name in ("section", "row", "col"))
    return jax.shard_map(
        functools.partial(per_device, sizes),
        mesh=mesh,
        in_specs=(
            P(None, None, None, "row", "col"),
            P(),
            P(),
            P("section", None, None),
            P("section", None, None),
            P("section", None, None),
            P("section", None, None),
            P("section", None, None),
            P("section", None, None, "row", "col"),
            P("section", None, None, "row", "col"),
            P(None, None, "row", "col"),
        ),
        out_specs=(
            P("section", None, None, "row", "col"),
            P("section", None, None, "row", "col"),
            P("section", None, None, "row", "col"),
        ),
        check_vma=False,
    )
```

time: 1280 us -> 212 us (0.17)
  starting transfers between devices: 649 us -> 0 us
  local copies, waits for them, and re-layouts: 295 us -> 31.6 us
  Pallas kernels: 0 us -> 167 us
  waiting for transfers between devices: 118 us -> 0 us
  other arithmetic: 105 us -> 12 us
  matrix products: 57.7 us -> 0.33 us
  loops' own time: 43.6 us -> 0 us
    ppermute x180 -> x0, starting transfers between devices: 649 us -> none  [the longest x72 323 us: extended(): lax.ppermute(tail, axis, [(i, (i + 1) % count) for i in range(ends)])]
    pallas_call x0 -> x1, Pallas kernels: none -> 167 us  [per_device(): pl.pallas_call(functools.partial(kernel_body, sections, rows, cols, steps...]
    dynamic_slice x108 -> x0, local copies, waits for them, and re-layouts: 151 us -> none  [the longest x36 37.3 us: advance(): frame_now = frames[moment, region_order[batch_index]]]
    ppermute x180 -> x0, waiting for transfers between devices: 118 us -> none  [the longest x18 79.1 us: passed_along(): return lax.ppermute(value, axis, pairs)]
    dot_general x48 -> x1, matrix products: 57.7 us -> 0.33 us  [per_device(): jnp.einsum('tbcyx,oc->tbyxo', picked, encoder, preferred_element_type=f32)]
    dynamic_update_slice x54 -> x0, other arithmetic: 56.2 us -> none  [the longest x18 31.6 us: advance(): lax.dynamic_update_index_in_dim(memory_last, jnp.where(active, memory_new...]
    another operation x110 -> x2, local copies, waits for them, and re-layouts: 45.8 us -> 0.5 us  [the longest x1 0.49 us: per_device(): ok = output_kernel[0].reshape(ch, KS, KS, 2 * ch).transpose(1, 2, 3, 0)]
    another operation x37 -> x0, loops' own time: 43.6 us -> none  [the longest x1 40.9 us: per_device(): lax.fori_loop(0, tick_count, advance, initial)]
  transfers between devices with their start and end apart: 180 -> 0, of which waited for: 39 -> 0; matrix products, arithmetic and copies ran while one was open for 15% -> 0% of each run, Pallas kernels for 0% -> 0%
where the time goes in v1:
time: 212 us
  Pallas kernels  167 us (79%)
  local copies, waits for them, and re-layouts  31.6 us (15%)
  other arithmetic  12 us (6%)
    pallas_call x1, Pallas kernels, per_device(): pl.pallas_call(functools.partial(kernel_body, sections, rows, cols, steps...  167 us
    concatenate x4, local copies, waits for them, and re-layouts, taps_first(): turned = jnp.concatenate(blocks, 0).transpose(1, 2, 3, 0)  11.5 us
    unnamed x40, local copies, waits for them, and re-layouts  7.17 us
    concatenate x1, other arithmetic, taps_first(): jnp.concatenate([turned[:, :4].reshape(-1, wide), turned[:, 4].reshape(-1...  6.03 us

profile of v1, /device:TPU:39, one launch (start us, length us, event | category | flops | bytes accessed | tf_op | source)
XLA Modules:
  0.0 211.8 jit_solution(210267418232171386)
XLA Ops:
  0.6 1.6 fusion.2
  2.7 1.0 copy.64
  3.7 1.0 copy.65
  4.7 1.0 copy.66
  5.9 1.0 copy.61
  6.8 3.7 %concatenate.51 = bf16[512,5,5,64]{0,3,2,1:T(8,128)(2,1)S(1)} concatenate(bf16[64,5,5,64]{0,3,2,1:T(8,128)(2,1)} %bitcast.79, bf16[64,5,5,64]{0,3,2,1:T(8,128)(2,1)S(1)} %bitcast.74, bf16[64,5,5,64]{0,3,2,1:T(8,128)(2,1)S(1)} %bitcast.75, bf16[64,5,5,64]{0,3,2,1:T(8,128)(2,1)} %bitcast.76, bf16[64,5,5,64]{0,3,2,1:T(8,128)(2,1)} %bitcast.77, bf16[64,5,5,64]{0,3,2,1:T(8,128)(2,1)} %bitcast.78, ...), dimensions={0} | concatenate | bytes 3276800 | tf_op jit(solution)/shard_map/concatenate | solution.py:374
  10.5 1.2 slice.124
  11.7 0.8 slice.125
  12.5 0.4 fusion.3
  12.9 0.8 copy.44
  13.7 0.8 copy.45
  14.6 3.5 %concatenate.53 = bf16[512,5,5,64]{0,3,1,2:T(8,128)(2,1)S(1)} concatenate(bf16[64,5,5,64]{0,3,1,2:T(8,128)(2,1)S(1)} %copy.43, bf16[64,5,5,64]{0,3,1,2:T(8,128)(2,1)S(1)} %broadcast_in_dim.28, bf16[64,5,5,64]{0,3,1,2:T(8,128)(2,1)} %copy.44, bf16[64,5,5,64]{0,3,1,2:T(8,128)(2,1)S(1)} %broadcast_in_dim.28, bf16[64,5,5,64]{0,3,1,2:T(8,128)(2,1)} %copy.45, ...), dimensions={0} | concatenate | bytes 3276800 | tf_op jit(solution)/shard_map/concatenate | solution.py:374
  18.2 1.1 copy.48
  19.4 0.7 slice.127
  21.0 0.8 copy.54
  21.8 0.8 concatenate.55
  22.6 3.4 %concatenate.56 = bf16[512,5,5,64]{0,3,1,2:T(8,128)(2,1)S(1)} concatenate(bf16[64,5,5,64]{0,3,1,2:T(8,128)(2,1)S(1)} %broadcast_in_dim.28, bf16[64,5,5,64]{0,3,1,2:T(8,128)(2,1)S(1)} %copy.52, bf16[64,5,5,64]{0,3,1,2:T(8,128)(2,1)S(1)} %broadcast_in_dim.28, bf16[64,5,5,64]{0,3,1,2:T(8,128)(2,1)S(1)} %copy.53, bf16[64,5,5,64]{0,3,1,2:T(8,128)(2,1)S(1)} %broadcast_in_dim.28, ...), dimensions={0} | concatenate | bytes 3276800 | tf_op jit(solution)/shard_map/concatenate | solution.py:374
  26.4 1.1 copy-done.1
  27.5 0.4 copy-done.2
  28.0 6.0 %maximum_maximum_fusion.2 = (bf16[1664,512]{1,0:T(8,128)(2,1)}, bf16[1664,512]{1,0:T(8,128)(2,1)}, bf16[1664,512]{1,0:T(8,128)(2,1)}) fusion(bf16[320,512]{1,0:T(8,128)(2,1)S(1)} %bitcast.90, bf16[1280,512]{1,0:T(8,128)(2,1)S(1)} %bitcast.67, bf16[1664]{0:T(1024)(128)(2,1)S(1)} %pad.15.clone, bf16[320,512]{1,0:T(8,128)(2,1)S(1)} %bitcast.89, ...), kind=kLoop, calls=%fused_computation.3 | loop fusion | flops 13631488 | bytes 10030336 | tf_op jit(solution)/shard_map/concatenate | solution.py:376
  34.1 0.5 reshape_squeeze.18
  34.8 0.3 copy.57
  35.4 1.6 pad_maximum_fusion.wo_ref
  37.0 0.6 gather_fusion
  37.7 0.3 convolution_convert_fusion
  38.1 1.0 pad_maximum_fusion.1
  39.0 0.9 pad_maximum_fusion.2.cel_ref
  40.0 0.8 pad_maximum_fusion.3.hid_ref
  40.8 0.8 pad_maximum_fusion.4.mem_ref
  41.7 0.7 maximum_bitcast_fusion.wmix_ref
  42.4 167.0 %predrnn.1 = (f32[3,8,32,128]{3,2,1,0:T(8,128)}, f32[3,8,32,128]{3,2,1,0:T(8,128)}) custom-call(bf16[6,8,32,128]{3,2,1,0:T(8,128)(2,1)} %bitcast.87, bf16[3,8,32,128]{3,2,1,0:T(8,128)(2,1)} %pad_maximum_fusion.3.hid_ref, f32[3,8,32,128]{3,2,1,0:T(8,128)} %pad_maximum_fusion.2.cel_ref, bf16[3,8,32,128]{3,2,1,0:T(8,128)(2,1)} %pad_maximum_fusion.4.mem_ref, ...), custom_call_target="tpu_custom_call" | custom-call | tf_op jit(solution)/shard_map/predrnn/pallas_call | solution.py:433
  209.4 2.4 %slice_bitcast_fusion = (f32[1,3,64,8,32]{2,4,3,1,0:T(8,128)}, f32[1,3,64,8,32]{2,4,3,1,0:T(8,128)}, f32[1,3,64,8,32]{2,4,3,1,0:T(8,128)}) fusion(f32[3,8,32,128]{3,2,1,0:T(8,128)} %get-tuple-element.6, f32[3,8,32,128]{3,2,1,0:T(8,128)} %get-tuple-element.5), kind=kLoop, calls=%fused_computation.8 | loop fusion | bytes 1179648 | tf_op jit(solution)/shard_map/broadcast_in_dim | solution.py:473
  (54 shorter events, 3.0 us)
Async XLA Ops:
  0.6 36.4 %copy-start = (bf16[2,6,16,8,32]{4,3,2,1,0:T(8,128)(2,1)S(1)}, bf16[2,6,16,8,32]{4,3,2,1,0:T(8,128)(2,1)}, u32[]{:S(2)}) copy-start(bf16[2,6,16,8,32]{4,3,2,1,0:T(8,128)(2,1)} %param.11) | copy-start | bytes 294916
  10.5 2.0 copy-start.3
  18.2 1.9 copy-start.6
  26.2 1.3 copy-start.1
  26.2 1.7 copy-start.2
  26.2 1.7 copy-start.4
  26.2 1.8 copy-start.5
  28.0 6.0 %copy-start.7 = (bf16[1,64,3200]{2,1,0:T(8,128)(2,1)S(1)}, bf16[1,64,3200]{2,1,0:T(8,128)(2,1)}, u32[]{:S(2)}) copy-start(bf16[1,64,3200]{2,1,0:T(8,128)(2,1)} %param.17) | copy-start | bytes 1228804
  34.7 2.2 %copy-start.13 = (s32[6]{0:T(128)S(1)}, s32[6]{0:T(128)}, u32[]{:S(2)}) copy-start(s32[6]{0:T(128)} %param.12) | copy-start | bytes 76
  35.0 2.6 %copy-start.12 = (bf16[64,16]{0,1:T(8,128)(2,1)S(1)}, bf16[64,16]{0,1:T(8,128)(2,1)}, u32[]{:S(2)}) copy-start(bf16[64,16]{0,1:T(8,128)(2,1)} %param.13) | copy-start | bytes 6148
  35.3 3.7 %copy-start.8 = (f32[1,3,64,8,32]{2,4,3,1,0:T(8,128)S(1)}, f32[1,3,64,8,32]{2,4,3,1,0:T(8,128)}, u32[]{:S(2)}) copy-start(f32[1,3,64,8,32]{2,4,3,1,0:T(8,128)} %param.20) | copy-start | bytes 589828
  37.0 3.0 %copy-start.9 = (f32[1,3,64,8,32]{2,4,3,1,0:T(8,128)S(1)}, f32[1,3,64,8,32]{2,4,3,1,0:T(8,128)}, u32[]{:S(2)}) copy-start(f32[1,3,64,8,32]{2,4,3,1,0:T(8,128)} %param.19) | copy-start | bytes 589828
  37.6 3.2 %copy-start.10 = (f32[3,64,8,32]{1,3,2,0:T(8,128)S(1)}, f32[3,64,8,32]{1,3,2,0:T(8,128)}, u32[]{:S(2)}) copy-start(f32[3,64,8,32]{1,3,2,0:T(8,128)} %param.21) | copy-start | bytes 589828
  38.0 3.6 %copy-start.11 = (bf16[1,64,128]{2,1,0:T(8,128)(2,1)S(1)}, bf16[1,64,128]{2,1,0:T(8,128)(2,1)}, u32[]{:S(2)}) copy-start(bf16[1,64,128]{2,1,0:T(8,128)(2,1)} %param.18) | copy-start | bytes 49156

commit v2 on v1

v2 whole, which is shorter than its diff:
```python
import functools

import jax
import jax.numpy as jnp
from jax import lax
from jax.experimental import pallas as pl
from jax.experimental.pallas import tpu as pltpu
from jax.sharding import PartitionSpec as P

KS = 5
HALO = 4
SIDE = 16
EDGE = 8
CH = 64
DIRS = [(-1, -1), (-1, 1), (1, -1), (1, 1), (0, -1), (0, 1), (-1, 0), (1, 0), (0, 0)]
AROUND = list(range(8))
EVERY = list(range(9))
MESH = pl.DeviceIdType.MESH

SLABS = {
    (0, 0): (0, 4, 8),
    (1, 0): (4, 0, 4),
    (-1, 0): (0, 12, 4),
    (0, 1): (13, 17, 2),
    (1, 1): (15, 16, 1),
    (-1, 1): (12, 19, 1),
    (0, -1): (9, 21, 2),
    (1, -1): (11, 20, 1),
    (-1, -1): (8, 23, 1),
}
STRIP_ROWS = [((0, 1), (2, 3)), ((0, 1), (4, 5)), ((2, 3), (6, 7)), ((4, 5), (6, 7))]
WINDOW_ROWS = [((0, 1), (2, 3)), ((4, 5), (8, 9)), ((6, 7), (10, 11)), ((12, 13), (14, 15))]


def sigmoid(value):
    return 0.5 * jnp.tanh(0.5 * value) + 0.5


def dot_last(left, right):
    return lax.dot_general(
        left, right, (((1,), (1,)), ((), ())), preferred_element_type=jnp.float32
    )


def kernel_body(
    sections,
    rows,
    cols,
    steps,
    batches,
    enc_ref,
    hid_ref,
    cel_ref,
    mem_ref,
    ik_ref,
    hk_ref,
    mk_ref,
    ok_ref,
    mix_ref,
    outh_ref,
    outs_ref,
    xwin,
    mwin,
    hwin,
    cwin,
    epack,
    hpack,
    cpack,
    mpack,
    hbuf,
    mbuf,
    wide,
    p01,
    p23,
    p40,
    p12,
    p34,
    acc_x,
    acc_h,
    acc_m,
    state,
    joined,
    js,
    wx,
    wh,
    wm,
    wo,
    wmix,
    w_sem,
    e_send,
    f_send,
    i_send,
    x_send,
    x_recv,
    m_send,
    m_recv,
    h_send,
    h_recv,
    c_send,
    c_recv,
    o_sem,
):
    bf16, f32 = jnp.bfloat16, jnp.float32
    sec = lax.axis_index("section")
    row = lax.axis_index("row")
    col = lax.axis_index("col")
    tr, tc = enc_ref.shape[1], enc_ref.shape[2]
    gr, gc = tr + 4, tc + 2 * EDGE
    wr = tr + 2 * HALO
    items = steps * batches
    first = sec == 0
    last = sec == sections - 1
    after = lax.rem(sec + 1, sections)
    before = lax.rem(sec + sections - 1, sections)

    def block(n, size=CH):
        return pl.ds(n * size, size)

    fetches = []

    def fetch(source, target):
        fetches.append(pltpu.make_async_copy(source, target, w_sem.at[len(fetches)]))

    fetch(hk_ref, wh)
    for place, gate in ((0, 1), (1, 0), (3, 2)):
        fetch(mk_ref.at[block(gate)], wm.at[block(place)])
    for place, gate in enumerate((0, 3, 1, 4, 2, 5, 6, 6)):
        fetch(ik_ref.at[block(gate)], wx.at[block(place)])
    half = KS * 2 * CH
    for p in range(KS):
        for copy in (0, 1):
            fetch(
                ok_ref.at[:, block(p, half)],
                wo.at[block(2 * (p % 2) + copy), block(p // 2, half)],
            )
    for copy in (0, 1):
        fetch(mix_ref, wmix.at[block(copy)])
    for copy in fetches:
        copy.start()

    def exists(dr, dc):
        found = None
        for ok in (
            row > 0 if dr < 0 else row < rows - 1 if dr > 0 else None,
            col > 0 if dc < 0 else col < cols - 1 if dc > 0 else None,
        ):
            if ok is not None:
                found = ok if found is None else found & ok
        return found

    def guarded(cond, fn):
        if cond is None:
            fn()
        else:
            pl.when(cond)(fn)

    def both(a, b):
        return b if a is None else a if b is None else a & b

    def copy_of(src, src_item, dst, dst_item, send_sem, recv_sem, target, index):
        dr, dc = DIRS[index]
        from_slab, to_slab, count = SLABS[(dr, dc)]
        return pltpu.make_async_remote_copy(
            src_ref=src.at[src_item, pl.ds(from_slab, count)],
            dst_ref=dst.at[dst_item, pl.ds(to_slab, count)],
            send_sem=send_sem.at[src_item, index],
            recv_sem=recv_sem.at[dst_item, index],
            device_id={
                "section": target,
                "row": lax.rem(row + dr + rows, rows),
                "col": lax.rem(col + dc + cols, cols),
            },
            device_id_type=MESH,
        )

    def each(indices, cond, fn):
        for index in indices:
            guarded(both(cond, exists(*DIRS[index])), functools.partial(fn, index))

    def each_source(indices, cond, fn):
        for index in indices:
            dr, dc = DIRS[index]
            guarded(both(cond, exists(-dr, -dc)), functools.partial(fn, index))

    def clear(k, _):
        zero = jnp.zeros(xwin.shape[1:], bf16)
        xwin[k] = zero
        mwin[k] = zero
        hwin[k] = zero
        return 0

    lax.fori_loop(0, items, clear, 0)

    def clear_cells(b, _):
        cwin[b] = jnp.zeros(cwin.shape[1:], bf16)
        return 0

    lax.fori_loop(0, batches, clear_cells, 0)

    barrier = pltpu.get_barrier_semaphore()
    for index in EVERY:
        dr, dc = DIRS[index]

        def greet(dr=dr, dc=dc):
            for target in (after, before) + (() if (dr, dc) == (0, 0) else (sec,)):
                pl.semaphore_signal(
                    barrier,
                    inc=1,
                    device_id={"section": target, "row": row + dr, "col": col + dc},
                    device_id_type=MESH,
                )

        guarded(exists(dr, dc), greet)

    js[:, gr] = jnp.zeros((KS, tc, 128), bf16)
    wide[...] = jnp.zeros(wide.shape, f32)
    wm[block(2), :] = jnp.zeros((CH, wm.shape[1]), bf16)
    wo[block(1, 2 * CH), block(2, half)] = jnp.zeros((2 * CH, half), bf16)

    low = lax.broadcasted_iota(jnp.int32, (1, 128), 1) < CH

    def pack(value_of, store):
        line = [value_of(r) for r in range(tr)]
        for r in range(tr):
            store(r, jnp.where(low, line[r][:16], line[r][16:32]).astype(bf16))
        for side, begin in ((8, 0), (12, tc - EDGE)):
            strip = [part[begin : begin + EDGE] for part in line]
            for slab, (lo, hi) in enumerate(STRIP_ROWS):
                upper = jnp.concatenate([strip[lo[0]], strip[lo[1]]], 0)
                lower = jnp.concatenate([strip[hi[0]], strip[hi[1]]], 0)
                store(side + slab, jnp.where(low, upper, lower).astype(bf16))

    def pack_into(target, item, value_of):
        def store(slab, value):
            target[item, slab] = value

        pack(value_of, store)

    def pack_first(b, _):
        pack_into(hpack, b, lambda r: hid_ref[b, r].astype(f32))
        pack_into(mpack, b, lambda r: mem_ref[b, r].astype(f32))
        pack_into(cpack, b, lambda r: cel_ref[b, r])
        return 0

    lax.fori_loop(0, batches, pack_first, 0)

    def pack_inputs(k, _):
        pack_into(epack, k, lambda r: enc_ref[k, r].astype(f32))
        return 0

    lax.fori_loop(0, items, pack_inputs, 0)

    near_rows = 1 + (row > 0).astype(jnp.int32) + (row < rows - 1).astype(jnp.int32)
    near_cols = 1 + (col > 0).astype(jnp.int32) + (col < cols - 1).astype(jnp.int32)
    pl.semaphore_wait(barrier, 3 * near_rows * near_cols - 1)

    def x_first(k, index):
        return copy_of(epack, k, xwin, k, e_send, x_recv, sec, index)

    def m_first(b, index):
        return copy_of(mpack, b, mwin, b, f_send, m_recv, sec, index)

    def h_first(b, index):
        return copy_of(hpack, b, hwin, b, i_send, h_recv, sec, index)

    def c_first(b, index):
        return copy_of(cpack, b, cwin, b, c_send, c_recv, sec, index)

    def x_next(k, index):
        return copy_of(hbuf, k, xwin, k, x_send, x_recv, after, index)

    def m_next(k, index):
        return copy_of(mbuf, k, mwin, k, m_send, m_recv, after, index)

    def m_loop(k, index):
        return copy_of(mbuf, k, mwin, k + batches, m_send, m_recv, after, index)

    def h_next(k, index):
        return copy_of(hbuf, k, hwin, k + batches, h_send, h_recv, sec, index)

    def own(src, src_item, dst, dst_item, sem):
        return pltpu.make_async_copy(
            src.at[src_item, pl.ds(0, tr)], dst.at[dst_item, pl.ds(HALO, tr)], sem
        )

    def x_own(k):
        return own(epack, k, xwin, k, o_sem.at[0, k])

    def m_own(b):
        return own(mpack, b, mwin, b, o_sem.at[1, b])

    def h_own_first(b):
        return own(hpack, b, hwin, b, o_sem.at[2, b])

    def h_own(b):
        return own(hbuf, b, hwin, b + batches, o_sem.at[3, b])

    def start(make, k):
        return lambda index: make(k, index).start()

    def sent(make, k):
        return lambda index: make(k, index).wait_send()

    def landed(make, k):
        return lambda index: make(k, index).wait_recv()

    def begin(b, _):
        each(AROUND, None, start(h_first, b))
        each(AROUND, first, start(m_first, b))
        each(AROUND, first, start(x_first, b))
        each(AROUND, None, start(c_first, b))
        h_own_first(b).start()

        @pl.when(first)
        def _():
            m_own(b).start()
            x_own(b).start()

        return 0

    lax.fori_loop(0, batches, begin, 0)

    def begin_later(k, _):
        each(AROUND, first, start(x_first, k))
        pl.when(first)(lambda: x_own(k).start())
        return 0

    lax.fori_loop(batches, items, begin_later, 0)
    for copy in fetches:
        copy.wait()

    def unpack(window):
        for r in range(wr):
            value = window[r].astype(f32)
            turned = pltpu.roll(value, CH, 1)
            wide[r, pl.ds(SIDE, 16), :] = jnp.where(low, value, turned)
            wide[r, pl.ds(SIDE + 16, 16), :] = jnp.where(low, turned, value)
        for base, column in ((wr, SIDE - EDGE), (wr + 4, SIDE + tc)):
            for slab, (lo, hi) in enumerate(WINDOW_ROWS):
                value = window[base + slab].astype(f32)
                turned = pltpu.roll(value, CH, 1)
                upper = jnp.where(low, value, turned)
                lower = jnp.where(low, turned, value)
                for n in (0, 1):
                    wide[lo[n], pl.ds(column, EDGE), :] = upper[n * EDGE : (n + 1) * EDGE]
                    wide[hi[n], pl.ds(column, EDGE), :] = lower[n * EDGE : (n + 1) * EDGE]

    def spread():
        def tap(r, q):
            return wide[r, pl.ds(SIDE - EDGE - 2 + q, gc), :]

        for r in range(wr):
            taps = [tap(r, q) for q in range(KS)]
            p01[r] = jnp.where(low, taps[0], taps[1]).astype(bf16)
            p23[r] = jnp.where(low, taps[2], taps[3]).astype(bf16)
            p12[r] = jnp.where(low, taps[1], taps[2]).astype(bf16)
            p34[r] = jnp.where(low, taps[3], taps[4]).astype(bf16)
            p40[r] = jnp.where(low, taps[4], tap(min(r + 1, wr - 1), 0)).astype(bf16)

    def patches():
        parts = []
        for p in (0, 2):
            for buffer, at in ((p01, p), (p23, p), (p40, p), (p12, p + 1), (p34, p + 1)):
                parts.append(buffer[at : at + gr].reshape(gr * gc, 128))
        parts.append(p01[4 : 4 + gr].reshape(gr * gc, 128))
        parts.append(p23[4 : 4 + gr].reshape(gr * gc, 128))
        parts.append(p40[4 : 4 + gr].reshape(gr * gc, 128)[:, :CH])
        return jnp.concatenate(parts, axis=1)

    def cell(k, _):
        b = lax.rem(k, batches)
        early = k < batches
        late = k >= batches

        each_source(AROUND, early, landed(h_first, b))
        each_source(AROUND, late, landed(h_next, b))
        pl.when(early)(lambda: h_own_first(b).wait())
        pl.when(late)(lambda: h_own(b).wait())
        unpack(hwin.at[k])
        spread()
        acc_h[...] = dot_last(patches(), wh[...])

        @pl.when(early)
        def _():
            each_source(AROUND, None, landed(c_first, b))
            unpack(cwin.at[b])
            for r in range(gr):
                state[b, r] = wide[r + HALO - 2, pl.ds(SIDE - EDGE, gc), :]
            for r in range(tr):
                state[b, r + 2, pl.ds(EDGE, tc), :] = cel_ref[b, r]

        each_source(AROUND, first & early, landed(m_first, b))
        pl.when(first & early)(lambda: m_own(b).wait())
        each_source(EVERY, jnp.logical_not(first) | late, landed(m_next, k))
        unpack(mwin.at[k])
        spread()
        acc_m[...] = dot_last(patches(), wm[...])
        for r in range(gr):
            memory = wide[r + HALO - 2, pl.ds(SIDE - EDGE, gc), :]
            state[b, r] = jnp.where(low, state[b, r], memory)

        each_source(AROUND, first, landed(x_first, k))
        pl.when(first)(lambda: x_own(k).wait())
        each_source(EVERY, jnp.logical_not(first), landed(x_next, k))
        unpack(xwin.at[k])
        spread()
        acc_x[...] = dot_last(patches(), wx[...])

        grid_col = lax.broadcasted_iota(jnp.int32, (gc, 1), 0) + (col * tc - EDGE)
        col_ok = (grid_col >= 0) & (grid_col < cols * tc)
        for r in range(gr):
            span = slice(r * gc, (r + 1) * gc)
            h0, h1 = acc_h[span, :128], acc_h[span, 128:]
            m0, m1 = acc_m[span, :128], acc_m[span, 128:]
            into = acc_x[span, :128] + jnp.where(low, h0, m0)
            keep = acc_x[span, 128:256] + pltpu.roll(jnp.where(low, m0, h0), CH, 1)
            fresh = acc_x[span, 256:384] + jnp.where(low, h1, m1)
            new = sigmoid(keep + 1.0) * state[b, r] + sigmoid(into) * jnp.tanh(fresh)
            state[b, r] = new
            grid_row = row * tr + (r - 2)
            ok = col_ok & ((grid_row >= 0) & (grid_row < rows * tr))
            joined[r] = jnp.where(ok, new, 0.0)

        def new_memory(r):
            value = state[b, r + 2, pl.ds(EDGE, tc), :]
            return jnp.where(low, pltpu.roll(value, CH, 1), value)

        pack_into(mbuf, k, new_memory)
        each(EVERY, jnp.logical_not(last), start(m_next, k))
        each(EVERY, last & early, start(m_loop, k))

        for q in range(KS):
            for r in range(gr):
                js[q, r] = joined[r, pl.ds(EDGE - 2 + q, tc), :].astype(bf16)
        parts = [
            js[q, 2 * g : 2 * g + tr + 1].reshape((tr + 1) * tc, 128)
            for g in range(3)
            for q in range(KS)
        ]
        out = dot_last(jnp.concatenate(parts, axis=1), wo[...])
        mixed = dot_last(js[2, 2 : 2 + tr].reshape(tr * tc, 128), wmix[...])
        hidden = []
        for r in range(tr):
            grid = slice((r + 2) * gc + EDGE, (r + 2) * gc + EDGE + tc)
            h1 = acc_h[grid, 128:]
            gate = out[r * tc : (r + 1) * tc, :128] + out[(r + 1) * tc : (r + 2) * tc, 128:]
            gate += acc_x[grid, 384:] + jnp.where(low, pltpu.roll(h1, CH, 1), h1)
            hidden.append(sigmoid(gate) * jnp.tanh(mixed[r * tc : (r + 1) * tc]))
        pack_into(hbuf, k, lambda r: hidden[r])
        each(EVERY, jnp.logical_not(last), start(x_next, k))

        @pl.when(early)
        def _():
            each(AROUND, None, start(h_next, k))
            h_own(k).start()

        @pl.when(late)
        def _():
            for r in range(tr):
                outh_ref[b, r] = hidden[r]
            outs_ref[b] = state[b, 2 : 2 + tr, EDGE : EDGE + tc, :]

        return 0

    lax.fori_loop(0, items, cell, 0)

    def finish(k, _):
        each(AROUND, first, sent(x_first, k))
        each(EVERY, jnp.logical_not(last), sent(x_next, k))
        each(EVERY, jnp.logical_not(last), sent(m_next, k))
        return 0

    def finish_early(b, _):
        each(AROUND, first, sent(m_first, b))
        each(EVERY, last, sent(m_loop, b))
        each(AROUND, None, sent(h_first, b))
        each(AROUND, None, sent(h_next, b))
        each(AROUND, None, sent(c_first, b))
        return 0

    lax.fori_loop(0, items, finish, 0)
    lax.fori_loop(0, batches, finish_early, 0)


def per_device(
    sizes,
    frames,
    region_order,
    encoder,
    input_kernel,
    hidden_kernel,
    memory_kernel,
    output_kernel,
    mixing_weight,
    hidden_start,
    cell_start,
    memory_start,
):
    bf16, f32 = jnp.bfloat16, jnp.float32
    sections, rows, cols = sizes
    steps, _, patch, tr, tc = frames.shape
    batches, ch = memory_start.shape[:2]
    items = steps * batches
    gr, gc = tr + 4, tc + 2 * EDGE
    wr, wc = tr + 2 * HALO, tc + 2 * SIDE
    taps = KS * KS * ch

    def twice(value):
        return jnp.concatenate([value, value], -1)

    picked = jnp.take(frames, region_order[:batches], axis=1)
    enc = jnp.einsum(
        "tbcyx,oc->tbyxo", picked, twice(encoder.T).T, preferred_element_type=f32
    )
    enc = enc.astype(bf16).reshape(items, tr, tc, 2 * ch)
    hid = twice(hidden_start[0].transpose(0, 2, 3, 1).astype(bf16))
    cel = twice(cell_start[0].transpose(0, 2, 3, 1))
    mem = twice(memory_start.transpose(0, 2, 3, 1).astype(bf16))

    vmem = pl.BlockSpec(memory_space=pltpu.VMEM)
    anywhere = pl.BlockSpec(memory_space=pl.ANY)
    dma = pltpu.SemaphoreType.DMA
    window, packed = (wr + 8, 16, 128), (tr + 8, 16, 128)
    ends = jax.ShapeDtypeStruct((batches, tr, tc, 2 * ch), f32)
    outh, outs = pl.pallas_call(
        functools.partial(kernel_body, sections, rows, cols, steps, batches),
        out_shape=(ends, ends),
        in_specs=[vmem] * 4 + [anywhere] * 5,
        out_specs=(vmem, vmem),
        scratch_shapes=[
            pltpu.VMEM((items,) + window, bf16),
            pltpu.VMEM((items,) + window, bf16),
            pltpu.VMEM((items,) + window, bf16),
            pltpu.VMEM((batches,) + window, bf16),
            pltpu.VMEM((items,) + packed, bf16),
            pltpu.VMEM((batches,) + packed, bf16),
            pltpu.VMEM((batches,) + packed, bf16),
            pltpu.VMEM((batches,) + packed, bf16),
            pltpu.VMEM((items,) + packed, bf16),
            pltpu.VMEM((items,) + packed, bf16),
            pltpu.VMEM((wr, wc, 128), f32),
        ]
        + [pltpu.VMEM((wr, gc, 128), bf16)] * 5
        + [
            pltpu.VMEM((gr * gc, 512), f32),
            pltpu.VMEM((gr * gc, 256), f32),
            pltpu.VMEM((gr * gc, 256), f32),
            pltpu.VMEM((batches, gr, gc, 128), f32),
            pltpu.VMEM((gr, gc, 128), f32),
            pltpu.VMEM((KS, gr + 1, tc, 128), bf16),
            pltpu.VMEM((8 * ch, taps), bf16),
            pltpu.VMEM((4 * ch, taps), bf16),
            pltpu.VMEM((4 * ch, taps), bf16),
            pltpu.VMEM((4 * ch, 3 * KS * 2 * ch), bf16),
            pltpu.VMEM((2 * ch, 2 * ch), bf16),
            dma((24,)),
            dma((items, 9)),
            dma((batches, 9)),
            dma((batches, 9)),
            dma((items, 9)),
            dma((items, 9)),
            dma((items, 9)),
            dma((items, 9)),
            dma((batches, 9)),
            dma((items, 9)),
            dma((batches, 9)),
            dma((batches, 9)),
            dma((4, items)),
        ],
        compiler_params=pltpu.CompilerParams(
            collective_id=0, has_side_effects=True, vmem_limit_bytes=48 << 20
        ),
        name="predrnn",
    )(
        enc,
        hid,
        cel,
        mem,
        input_kernel[0],
        hidden_kernel[0],
        memory_kernel[0],
        output_kernel[0],
        mixing_weight[0],
    )

    def back(value):
        return value.transpose(0, 3, 1, 2)[None]

    return back(outh[..., :ch]), back(outs[..., :ch]), back(outs[..., ch:])


def solution(mesh):
    sizes = tuple(mesh.shape[name] for name in ("section", "row", "col"))
    return jax.shard_map(
        functools.partial(per_device, sizes),
        mesh=mesh,
        in_specs=(
            P(None, None, None, "row", "col"),
            P(),
            P(),
            P("section", None, None),
            P("section", None, None),
            P("section", None, None),
            P("section", None, None),
            P("section", None, None),
            P("section", None, None, "row", "col"),
            P("section", None, None, "row", "col"),
            P(None, None, "row", "col"),
        ),
        out_specs=(
            P("section", None, None, "row", "col"),
            P("section", None, None, "row", "col"),
            P("section", None, None, "row", "col"),
        ),
        check_vma=False,
    )
```

time: 212 us -> 142 us (0.67)
  Pallas kernels: 167 us -> 130 us
  local copies, waits for them, and re-layouts: 31.6 us -> 7.46 us
  other arithmetic: 12 us -> 2.68 us
    pallas_call x1, Pallas kernels: 167 us -> 130 us  [per_device(): pl.pallas_call(functools.partial(kernel_body, sections, rows, cols, steps...]
    concatenate x6 -> x0, local copies, waits for them, and re-layouts: 11.6 us -> none  [the longest x4 11.5 us: taps_first(): turned = jnp.concatenate(blocks, 0).transpose(1, 2, 3, 0)]
    concatenate x2 -> x0, other arithmetic: 7.63 us -> none  [the longest x1 6.03 us: taps_first(): jnp.concatenate([turned[:, :4].reshape(-1, wide), turned[:, 4].reshape(-1...]
    slice x14 -> x0, local copies, waits for them, and re-layouts: 6.74 us -> none  [the longest x5 2.6 us: taps_first(): turned[:, :4].reshape(-1, wide)]
    squeeze x7 -> x0, local copies, waits for them, and re-layouts: 2.52 us -> none  [the longest x4 1.65 us: per_device(): wh = taps_first([hk[0], none, hk[1], none, hk[2], none, hk[3], hk[3]])]
    unnamed x40 -> x21, local copies, waits for them, and re-layouts: 7.17 us -> 5.82 us
where the time goes in v2:
time: 142 us
  Pallas kernels  130 us (92%)
  local copies, waits for them, and re-layouts  7.46 us (5%)
  other arithmetic  2.68 us (2%)
    pallas_call x1, Pallas kernels, per_device(): pl.pallas_call(functools.partial(kernel_body, sections, rows, cols, steps...  130 us
    unnamed x21, local copies, waits for them, and re-layouts  5.82 us

profile of v2, /device:TPU:39, one launch (start us, length us, event | category | flops | bytes accessed | tf_op | source)
XLA Modules:
  0.0 141.9 jit_solution(9917188184176187142)
XLA Ops:
  0.6 0.0 copy-start
  0.6 0.0 copy-start.8
  0.7 0.0 copy-start.7
  0.7 0.8 compare_and_fusion
  1.4 0.3 copy-done
  1.8 0.6 gather_fusion
  2.4 0.0 copy-start.9
  2.4 0.1 select_bitcast_fusion
  2.5 1.1 convolution_convert_fusion
  3.6 0.0 copy-done.7
  3.6 0.8 pad_maximum_fusion.1.hid_ref
  4.4 0.0 copy-done.8
  4.5 0.0 copy-start.1
  4.5 0.0 copy-start.6
  4.5 0.8 pad_maximum_fusion.2.mem_ref
  5.3 0.0 copy-done.9
  5.3 0.2 pad_maximum_fusion.cel_ref
  5.5 1.5 %copy.15 = bf16[1,256,1600]{2,1,0:T(8,128)(2,1)S(1)} copy(bf16[1,256,1600]{1,2,0:T(8,128)(2,1)} %param.15) | data formatting | bytes 1638400 | tf_op args[4]
  7.0 0.0 copy-done.1
  7.0 0.0 copy-done.6
  7.0 0.0 copy-start.2
  7.0 0.9 copy-done.2
  7.9 0.0 copy-start.3
  8.0 0.9 copy-done.3
  8.9 0.0 copy-start.4
  8.9 1.1 copy-done.4
  10.0 0.0 copy-start.5
  10.0 1.0 copy-done.5
  11.0 129.9 %predrnn.1 = (f32[3,8,32,128]{3,2,1,0:T(8,128)S(1)}, f32[3,8,32,128]{3,2,1,0:T(8,128)S(1)}) custom-call(bf16[6,8,32,128]{3,2,1,0:T(8,128)(2,1)S(1)} %bitcast.36, bf16[3,8,32,128]{3,2,1,0:T(8,128)(2,1)S(1)} %copy-done.2, f32[3,8,32,128]{3,2,1,0:T(8,128)S(1)} %pad_maximum_fusion.cel_ref, bf16[3,8,32,128]{3,2,1,0:T(8,128)(2,1)S(1)} %copy-done.3, ...), custom_call_target="tpu_custom_call" | custom-call | tf_op jit(solution)/shard_map/predrnn/pallas_call | solution.py:525
  140.9 1.1 slice_bitcast_fusion
  (3 shorter events, 0.1 us)
Async XLA Ops:
  0.6 1.1 copy-start
  0.6 3.8 %copy-start.8 = (f32[3,64,8,32]{1,3,2,0:T(8,128)S(1)}, f32[3,64,8,32]{1,3,2,0:T(8,128)}, u32[]{:S(2)}) copy-start(f32[3,64,8,32]{1,3,2,0:T(8,128)} %param.21) | copy-start | bytes 589828
  0.7 2.9 %copy-start.7 = (f32[1,3,64,8,32]{2,4,3,1,0:T(8,128)S(1)}, f32[1,3,64,8,32]{2,4,3,1,0:T(8,128)}, u32[]{:S(2)}) copy-start(f32[1,3,64,8,32]{2,4,3,1,0:T(8,128)} %param.19) | copy-start | bytes 589828
  2.4 2.9 %copy-start.9 = (f32[1,3,64,8,32]{2,4,3,1,0:T(8,128)S(1)}, f32[1,3,64,8,32]{2,4,3,1,0:T(8,128)}, u32[]{:S(2)}) copy-start(f32[1,3,64,8,32]{2,4,3,1,0:T(8,128)} %param.20) | copy-start | bytes 589828
  4.5 2.5 %copy-start.1 = (bf16[1,448,1600]{2,1,0:T(8,128)(2,1)S(1)}, bf16[1,448,1600]{2,1,0:T(8,128)(2,1)}, u32[]{:S(2)}) copy-start(bf16[1,448,1600]{2,1,0:T(8,128)(2,1)} %param.14) | copy-start | bytes 4300804
  4.5 2.5 %copy-start.6 = (bf16[1,64,128]{2,1,0:T(8,128)(2,1)S(1)}, bf16[1,64,128]{2,1,0:T(8,128)(2,1)}, u32[]{:S(2)}) copy-start(bf16[1,64,128]{2,1,0:T(8,128)(2,1)} %param.18) | copy-start | bytes 49156
  7.0 0.9 copy-start.2
  7.9 0.9 copy-start.3
  8.9 1.1 copy-start.4
  10.0 1.0 copy-start.5

commit v3 on v2

--- a/solution.py
+++ b/solution.py
@@ -37,9 +37,12 @@
 
 
 def dot_last(left, right):
-    return lax.dot_general(
-        left, right, (((1,), (1,)), ((), ())), preferred_element_type=jnp.float32
-    )
+    def part(a, b):
+        return lax.dot_general(a, b, (((1,), (1,)), ((), ())), preferred_element_type=jnp.float32)
+
+    if left.shape[1] < 1600:
+        return part(left, right)
+    return jnp.concatenate([part(left[:288], right), part(left[288:], right)], 0)
 
 
 def kernel_body(
@@ -48,10 +51,10 @@
     cols,
     steps,
     batches,
-    enc_ref,
-    hid_ref,
-    cel_ref,
-    mem_ref,
+    enc_in,
+    hid_in,
+    cel_in,
+    mem_in,
     ik_ref,
     hk_ref,
     mk_ref,
@@ -75,13 +78,19 @@
     p40,
     p12,
     p34,
-    acc_x,
     acc_h,
     acc_m,
     state,
+    memory,
+    fresh_memory,
     joined,
     js,
-    wx,
+    enc_ref,
+    hid_ref,
+    cel_ref,
+    mem_ref,
+    wxm,
+    wxc,
     wh,
     wm,
     wo,
@@ -104,7 +113,7 @@
     sec = lax.axis_index("section")
     row = lax.axis_index("row")
     col = lax.axis_index("col")
-    tr, tc = enc_ref.shape[1], enc_ref.shape[2]
+    tr, tc = enc_in.shape[1], enc_in.shape[2]
     gr, gc = tr + 4, tc + 2 * EDGE
     wr = tr + 2 * HALO
     items = steps * batches
@@ -113,30 +122,34 @@
     after = lax.rem(sec + 1, sections)
     before = lax.rem(sec + sections - 1, sections)
 
-    def block(n, size=CH):
-        return pl.ds(n * size, size)
-
+    half = KS * 2 * CH
     fetches = []
 
     def fetch(source, target):
-        fetches.append(pltpu.make_async_copy(source, target, w_sem.at[len(fetches)]))
-
-    fetch(hk_ref, wh)
-    for place, gate in ((0, 1), (1, 0), (3, 2)):
-        fetch(mk_ref.at[block(gate)], wm.at[block(place)])
-    for place, gate in enumerate((0, 3, 1, 4, 2, 5, 6, 6)):
-        fetch(ik_ref.at[block(gate)], wx.at[block(place)])
-    half = KS * 2 * CH
-    for p in range(KS):
-        for copy in (0, 1):
-            fetch(
-                ok_ref.at[:, block(p, half)],
-                wo.at[block(2 * (p % 2) + copy), block(p // 2, half)],
-            )
-    for copy in (0, 1):
-        fetch(mix_ref, wmix.at[block(copy)])
-    for copy in fetches:
+        copy = pltpu.make_async_copy(source, target, w_sem.at[len(fetches)])
         copy.start()
+        fetches.append(copy)
+        return copy
+
+    in_hid = fetch(hid_in, hid_ref)
+    in_mem = fetch(mem_in, mem_ref)
+    in_enc = fetch(enc_in, enc_ref)
+    in_cel = fetch(cel_in, cel_ref)
+    in_wh = [fetch(hk_ref, wh)]
+    in_wm = [fetch(mk_ref, wm.at[pl.ds(0, 3 * CH)])]
+    in_wxm = [fetch(ik_ref.at[pl.ds(3 * CH, 3 * CH)], wxm.at[pl.ds(0, 3 * CH)])]
+    in_wxc = [
+        fetch(ik_ref.at[pl.ds(0, 3 * CH)], wxc.at[pl.ds(0, 3 * CH)]),
+        fetch(ik_ref.at[pl.ds(6 * CH, CH)], wxc.at[pl.ds(3 * CH, CH)]),
+    ]
+    in_wo = [
+        fetch(
+            ok_ref.at[:, pl.ds(p * half, half)],
+            wo.at[pl.ds(p % 4 * CH, CH), pl.ds(p // 4 * half, half)],
+        )
+        for p in range(KS)
+    ]
+    in_wo += [fetch(mix_ref, wmix.at[pl.ds(copy * CH, CH)]) for copy in (0, 1)]
 
     def exists(dr, dc):
         found = None
@@ -212,40 +225,49 @@
 
         guarded(exists(dr, dc), greet)
 
-    js[:, gr] = jnp.zeros((KS, tc, 128), bf16)
+    js[:, gr:] = jnp.zeros((KS, 3, tc, 128), bf16)
     wide[...] = jnp.zeros(wide.shape, f32)
-    wm[block(2), :] = jnp.zeros((CH, wm.shape[1]), bf16)
-    wo[block(1, 2 * CH), block(2, half)] = jnp.zeros((2 * CH, half), bf16)
+    for target in (wm, wxm):
+        target[3 * CH :, :] = jnp.zeros((CH, target.shape[1]), bf16)
+    wo[CH:, half:] = jnp.zeros((3 * CH, half), bf16)
 
     low = lax.broadcasted_iota(jnp.int32, (1, 128), 1) < CH
 
-    def pack(value_of, store):
+    def turn(value):
+        return pltpu.roll(value, CH, 1)
+
+    def pack_into(target, item, value_of, merge):
         line = [value_of(r) for r in range(tr)]
         for r in range(tr):
-            store(r, jnp.where(low, line[r][:16], line[r][16:32]).astype(bf16))
+            target[item, r] = merge(line[r][:16], line[r][16:32]).astype(bf16)
         for side, begin in ((8, 0), (12, tc - EDGE)):
             strip = [part[begin : begin + EDGE] for part in line]
             for slab, (lo, hi) in enumerate(STRIP_ROWS):
                 upper = jnp.concatenate([strip[lo[0]], strip[lo[1]]], 0)
                 lower = jnp.concatenate([strip[hi[0]], strip[hi[1]]], 0)
-                store(side + slab, jnp.where(low, upper, lower).astype(bf16))
-
-    def pack_into(target, item, value_of):
-        def store(slab, value):
-            target[item, slab] = value
-
-        pack(value_of, store)
+                target[item, side + slab] = merge(upper, lower).astype(bf16)
+
+    def merge_alike(one, two):
+        return jnp.where(low, one, two)
+
+    def merge_low(one, two):
+        return jnp.where(low, one, turn(two))
+
+    def merge_high(one, two):
+        return jnp.where(low, turn(one), two)
 
     def pack_first(b, _):
-        pack_into(hpack, b, lambda r: hid_ref[b, r].astype(f32))
-        pack_into(mpack, b, lambda r: mem_ref[b, r].astype(f32))
-        pack_into(cpack, b, lambda r: cel_ref[b, r])
-        return 0
-
+        pack_into(hpack, b, lambda r: hid_ref[b, r].astype(f32), merge_alike)
+        pack_into(mpack, b, lambda r: mem_ref[b, r].astype(f32), merge_alike)
+        pack_into(cpack, b, lambda r: cel_ref[b, r], merge_alike)
+        return 0
+
+    for copy in (in_hid, in_mem, in_cel, in_enc):
+        copy.wait()
     lax.fori_loop(0, batches, pack_first, 0)
 
     def pack_inputs(k, _):
-        pack_into(epack, k, lambda r: enc_ref[k, r].astype(f32))
+        pack_into(epack, k, lambda r: enc_ref[k, r].astype(f32), merge_alike)
         return 0
 
     lax.fori_loop(0, items, pack_inputs, 0)
@@ -326,9 +348,6 @@
         return 0
 
     lax.fori_loop(batches, items, begin_later, 0)
-    for copy in fetches:
-        copy.wait()
-
     def unpack(window):
         for r in range(wr):
             value = window[r].astype(f32)
@@ -367,6 +386,14 @@
         parts.append(p40[4 : 4 + gr].reshape(gr * gc, 128)[:, :CH])
         return jnp.concatenate(parts, axis=1)
 
+    def arrived(k, copies):
+        @pl.when(k == 0)
+        def _():
+            for copy in copies:
+                copy.wait()
+
+    bias = jnp.where(low, 0.0, 1.0)
+
     def cell(k, _):
         b = lax.rem(k, batches)
         early = k < batches
@@ -376,6 +403,7 @@
         each_source(AROUND, late, landed(h_next, b))
         pl.when(early)(lambda: h_own_first(b).wait())
         pl.when(late)(lambda: h_own(b).wait())
+        arrived(k, in_wh)
         unpack(hwin.at[k])
         spread()
         acc_h[...] = dot_last(patches(), wh[...])
@@ -392,49 +420,48 @@
         each_source(AROUND, first & early, landed(m_first, b))
         pl.when(first & early)(lambda: m_own(b).wait())
         each_source(EVERY, jnp.logical_not(first) | late, landed(m_next, k))
+        arrived(k, in_wm)
         unpack(mwin.at[k])
         spread()
         acc_m[...] = dot_last(patches(), wm[...])
         for r in range(gr):
-            memory = wide[r + HALO - 2, pl.ds(SIDE - EDGE, gc), :]
-            state[b, r] = jnp.where(low, state[b, r], memory)
+            memory[r] = wide[r + HALO - 2, pl.ds(SIDE - EDGE, gc), :]
 
         each_source(AROUND, first, landed(x_first, k))
         pl.when(first)(lambda: x_own(k).wait())
         each_source(EVERY, jnp.logical_not(first), landed(x_next, k))
+        arrived(k, in_wxm + in_wxc)
         unpack(xwin.at[k])
         spread()
-        acc_x[...] = dot_last(patches(), wx[...])
+        acc_m[...] += dot_last(patches(), wxm[...])
+        acc_h[...] += dot_last(patches(), wxc[...])
+
+        for r in range(gr):
+            span = slice(r * gc, (r + 1) * gc)
+            gates = sigmoid(acc_m[span, :128] + bias)
+            fresh_memory[r] = turn(gates) * memory[r] + gates * jnp.tanh(acc_m[span, 128:])
+        pack_into(mbuf, k, lambda r: fresh_memory[r + 2, pl.ds(EDGE, tc), :], merge_low)
+        each(EVERY, jnp.logical_not(last), start(m_next, k))
+        each(EVERY, last & early, start(m_loop, k))
 
         grid_col = lax.broadcasted_iota(jnp.int32, (gc, 1), 0) + (col * tc - EDGE)
         col_ok = (grid_col >= 0) & (grid_col < cols * tc)
         for r in range(gr):
             span = slice(r * gc, (r + 1) * gc)
-            h0, h1 = acc_h[span, :128], acc_h[span, 128:]
-            m0, m1 = acc_m[span, :128], acc_m[span, 128:]
-            into = acc_x[span, :128] + jnp.where(low, h0, m0)
-            keep = acc_x[span, 128:256] + pltpu.roll(jnp.where(low, m0, h0), CH, 1)
-            fresh = acc_x[span, 256:384] + jnp.where(low, h1, m1)
-            new = sigmoid(keep + 1.0) * state[b, r] + sigmoid(into) * jnp.tanh(fresh)
+            gates = sigmoid(acc_h[span, :128] + bias)
+            new = turn(gates) * state[b, r] + gates * jnp.tanh(acc_h[span, 128:])
             state[b, r] = new
             grid_row = row * tr + (r - 2)
             ok = col_ok & ((grid_row >= 0) & (grid_row < rows * tr))
-            joined[r] = jnp.where(ok, new, 0.0)
-
-        def new_memory(r):
-            value = state[b, r + 2, pl.ds(EDGE, tc), :]
-            return jnp.where(low, pltpu.roll(value, CH, 1), value)
-
-        pack_into(mbuf, k, new_memory)
-        each(EVERY, jnp.logical_not(last), start(m_next, k))
-        each(EVERY, last & early, start(m_loop, k))
-
+            joined[r] = jnp.where(ok, jnp.where(low, new, turn(fresh_memory[r])), 0.0)
+
+        arrived(k, in_wo)
         for q in range(KS):
             for r in range(gr):
                 js[q, r] = joined[r, pl.ds(EDGE - 2 + q, tc), :].astype(bf16)
         parts = [
-            js[q, 2 * g : 2 * g + tr + 1].reshape((tr + 1) * tc, 128)
-            for g in range(3)
+            js[q, 4 * g : 4 * g + tr + 3].reshape((tr + 3) * tc, 128)
+            for g in range(2)
             for q in range(KS)
         ]
         out = dot_last(jnp.concatenate(parts, axis=1), wo[...])
@@ -442,11 +469,11 @@
         hidden = []
         for r in range(tr):
             grid = slice((r + 2) * gc + EDGE, (r + 2) * gc + EDGE + tc)
-            h1 = acc_h[grid, 128:]
-            gate = out[r * tc : (r + 1) * tc, :128] + out[(r + 1) * tc : (r + 2) * tc, 128:]
-            gate += acc_x[grid, 384:] + jnp.where(low, pltpu.roll(h1, CH, 1), h1)
+            line = [slice((r + n) * tc, (r + n + 1) * tc) for n in range(4)]
+            gate = out[line[1], :128] + out[line[3], 128:] + acc_h[grid, 128:]
+            gate += turn(out[line[0], :128] + out[line[2], 128:])
             hidden.append(sigmoid(gate) * jnp.tanh(mixed[r * tc : (r + 1) * tc]))
-        pack_into(hbuf, k, lambda r: hidden[r])
+        pack_into(hbuf, k, lambda r: hidden[r], merge_high)
         each(EVERY, jnp.logical_not(last), start(x_next, k))
 
         @pl.when(early)
@@ -458,7 +485,7 @@
         def _():
             for r in range(tr):
                 outh_ref[b, r] = hidden[r]
-            outs_ref[b] = state[b, 2 : 2 + tr, EDGE : EDGE + tc, :]
+            outs_ref[b] = joined[2 : 2 + tr, EDGE : EDGE + tc, :]
 
         return 0
 
@@ -525,7 +552,7 @@
     outh, outs = pl.pallas_call(
         functools.partial(kernel_body, sections, rows, cols, steps, batches),
         out_shape=(ends, ends),
-        in_specs=[vmem] * 4 + [anywhere] * 5,
+        in_specs=[anywhere] * 9,
         out_specs=(vmem, vmem),
         scratch_shapes=[
             pltpu.VMEM((items,) + window, bf16),
@@ -542,16 +569,22 @@
         ]
         + [pltpu.VMEM((wr, gc, 128), bf16)] * 5
         + [
-            pltpu.VMEM((gr * gc, 512), f32),
             pltpu.VMEM((gr * gc, 256), f32),
             pltpu.VMEM((gr * gc, 256), f32),
             pltpu.VMEM((batches, gr, gc, 128), f32),
             pltpu.VMEM((gr, gc, 128), f32),
-            pltpu.VMEM((KS, gr + 1, tc, 128), bf16),
-            pltpu.VMEM((8 * ch, taps), bf16),
+            pltpu.VMEM((gr, gc, 128), f32),
+            pltpu.VMEM((gr, gc, 128), f32),
+            pltpu.VMEM((KS, gr + 3, tc, 128), bf16),
+            pltpu.VMEM(enc.shape, bf16),
+            pltpu.VMEM(hid.shape, bf16),
+            pltpu.VMEM(cel.shape, f32),
+            pltpu.VMEM(mem.shape, bf16),
             pltpu.VMEM((4 * ch, taps), bf16),
             pltpu.VMEM((4 * ch, taps), bf16),
-            pltpu.VMEM((4 * ch, 3 * KS * 2 * ch), bf16),
+            pltpu.VMEM((4 * ch, taps), bf16),
+            pltpu.VMEM((4 * ch, taps), bf16),
+            pltpu.VMEM((4 * ch, 2 * KS * 2 * ch), bf16),
             pltpu.VMEM((2 * ch, 2 * ch), bf16),
             dma((24,)),
             dma((items, 9)),
@@ -586,7 +619,7 @@
     def back(value):
         return value.transpose(0, 3, 1, 2)[None]
 
-    return back(outh[..., :ch]), back(outs[..., :ch]), back(outs[..., ch:])
+    return back(outh[..., ch:]), back(outs[..., :ch]), back(outs[..., ch:])
 
 
 def solution(mesh):

time: 142 us -> 130 us (0.915)
  Pallas kernels: 130 us -> 118 us
    pallas_call x1, Pallas kernels: 130 us -> 118 us  [per_device(): pl.pallas_call(functools.partial(kernel_body, sections, rows, cols, steps...]
where the time goes in v3:
time: 130 us
  Pallas kernels  118 us (91%)
  local copies, waits for them, and re-layouts  7.62 us (6%)
  other arithmetic  2.68 us (2%)
    pallas_call x1, Pallas kernels, per_device(): pl.pallas_call(functools.partial(kernel_body, sections, rows, cols, steps...  118 us
    unnamed x21, local copies, waits for them, and re-layouts  5.82 us

profile of v3, /device:TPU:39, one launch (start us, length us, event | category | flops | bytes accessed | tf_op | source)
XLA Modules:
  0.0 130.0 jit_solution(1973356563374048340)
XLA Ops:
  0.6 0.0 copy-start
  0.6 0.0 copy-start.8
  0.7 0.0 copy-start.7
  0.7 0.8 compare_and_fusion
  1.4 0.3 copy-done
  1.8 0.6 gather_fusion
  2.4 0.0 copy-start.9
  2.4 0.1 select_bitcast_fusion
  2.5 1.1 convolution_convert_fusion
  3.6 0.0 copy-done.7
  3.6 0.8 pad_maximum_fusion.1.hid_in
  4.4 0.0 copy-done.8
  4.5 0.0 copy-start.1
  4.5 0.0 copy-start.6
  4.5 0.8 pad_maximum_fusion.2.mem_in
  5.3 0.0 copy-done.9
  5.3 0.2 pad_maximum_fusion.cel_in
  5.5 1.5 %copy.15 = bf16[1,256,1600]{2,1,0:T(8,128)(2,1)S(1)} copy(bf16[1,256,1600]{1,2,0:T(8,128)(2,1)} %param.15) | data formatting | bytes 1638400 | tf_op args[4]
  7.0 0.0 copy-done.1
  7.0 0.0 copy-done.6
  7.0 0.0 copy-start.2
  7.0 0.9 copy-done.2
  7.9 0.0 copy-start.3
  8.0 0.9 copy-done.3
  8.9 0.0 copy-start.4
  8.9 1.1 copy-done.4
  10.0 0.0 copy-start.5
  10.0 1.0 copy-done.5
  11.0 117.8 %predrnn.1 = (f32[3,8,32,128]{3,2,1,0:T(8,128)S(1)}, f32[3,8,32,128]{3,2,1,0:T(8,128)S(1)}) custom-call(bf16[6,8,32,128]{3,2,1,0:T(8,128)(2,1)S(1)} %bitcast.36, bf16[3,8,32,128]{3,2,1,0:T(8,128)(2,1)S(1)} %copy-done.2, f32[3,8,32,128]{3,2,1,0:T(8,128)S(1)} %pad_maximum_fusion.cel_in, bf16[3,8,32,128]{3,2,1,0:T(8,128)(2,1)S(1)} %copy-done.3, ...), custom_call_target="tpu_custom_call" | custom-call | tf_op jit(solution)/shard_map/predrnn/pallas_call | solution.py:552
  128.8 1.2 slice_bitcast_fusion
  (3 shorter events, 0.1 us)
Async XLA Ops:
  0.6 1.1 copy-start
  0.6 3.8 %copy-start.8 = (f32[3,64,8,32]{1,3,2,0:T(8,128)S(1)}, f32[3,64,8,32]{1,3,2,0:T(8,128)}, u32[]{:S(2)}) copy-start(f32[3,64,8,32]{1,3,2,0:T(8,128)} %param.21) | copy-start | bytes 589828
  0.7 2.9 %copy-start.7 = (f32[1,3,64,8,32]{2,4,3,1,0:T(8,128)S(1)}, f32[1,3,64,8,32]{2,4,3,1,0:T(8,128)}, u32[]{:S(2)}) copy-start(f32[1,3,64,8,32]{2,4,3,1,0:T(8,128)} %param.19) | copy-start | bytes 589828
  2.4 2.9 %copy-start.9 = (f32[1,3,64,8,32]{2,4,3,1,0:T(8,128)S(1)}, f32[1,3,64,8,32]{2,4,3,1,0:T(8,128)}, u32[]{:S(2)}) copy-start(f32[1,3,64,8,32]{2,4,3,1,0:T(8,128)} %param.20) | copy-start | bytes 589828
  4.5 2.5 %copy-start.1 = (bf16[1,448,1600]{2,1,0:T(8,128)(2,1)S(1)}, bf16[1,448,1600]{2,1,0:T(8,128)(2,1)}, u32[]{:S(2)}) copy-start(bf16[1,448,1600]{2,1,0:T(8,128)(2,1)} %param.14) | copy-start | bytes 4300804
  4.5 2.5 %copy-start.6 = (bf16[1,64,128]{2,1,0:T(8,128)(2,1)S(1)}, bf16[1,64,128]{2,1,0:T(8,128)(2,1)}, u32[]{:S(2)}) copy-start(bf16[1,64,128]{2,1,0:T(8,128)(2,1)} %param.18) | copy-start | bytes 49156
  7.0 0.9 copy-start.2
  7.9 0.9 copy-start.3
  8.9 1.1 copy-start.4
  10.0 1.0 copy-start.5

commit v4 on v3

--- a/solution.py
+++ b/solution.py
@@ -43,6 +43,17 @@
     if left.shape[1] < 1600:
         return part(left, right)
     return jnp.concatenate([part(left[:288], right), part(left[288:], right)], 0)
+
+
+def dot_rows(left, right):
+    half = left.shape[0] // 2
+    return jnp.concatenate(
+        [
+            jnp.dot(part, right, preferred_element_type=jnp.float32)
+            for part in (left[:half], left[half:])
+        ],
+        0,
+    )
 
 
 def kernel_body(
@@ -406,7 +417,7 @@
         arrived(k, in_wh)
         unpack(hwin.at[k])
         spread()
-        acc_h[...] = dot_last(patches(), wh[...])
+        acc_h[...] = dot_rows(patches(), wh[...])
 
         @pl.when(early)
         def _():
@@ -582,7 +593,7 @@
             pltpu.VMEM(mem.shape, bf16),
             pltpu.VMEM((4 * ch, taps), bf16),
             pltpu.VMEM((4 * ch, taps), bf16),
-            pltpu.VMEM((4 * ch, taps), bf16),
+            pltpu.VMEM((taps, 4 * ch), bf16),
             pltpu.VMEM((4 * ch, taps), bf16),
             pltpu.VMEM((4 * ch, 2 * KS * 2 * ch), bf16),
             pltpu.VMEM((2 * ch, 2 * ch), bf16),
@@ -601,7 +612,7 @@
             dma((4, items)),
         ],
         compiler_params=pltpu.CompilerParams(
-            collective_id=0, has_side_effects=True, vmem_limit_bytes=48 << 20
+            collective_id=0, has_side_effects=True, vmem_limit_bytes=67_043_328
         ),
         name="predrnn",
     )(
@@ -610,7 +621,7 @@
         cel,
         mem,
         input_kernel[0],
-        hidden_kernel[0],
+        hidden_kernel[0].T,
         memory_kernel[0],
         output_kernel[0],
         mixing_weight[0],

time: 130 us -> 127 us (0.977)
  local copies, waits for them, and re-layouts: 7.62 us -> 4.06 us
    unnamed x21 -> x6, local copies, waits for them, and re-layouts: 5.82 us -> 0.01 us
where the time goes in v4:
time: 127 us
  Pallas kernels  117 us (92%)
  local copies, waits for them, and re-layouts  4.06 us (3%)
  other arithmetic  3.41 us (3%)
  matrix products  1.86 us (1%)
    pallas_call x1, Pallas kernels, per_device(): pl.pallas_call(functools.partial(kernel_body, sections, rows, cols, steps...  117 us

profile of v4, /device:TPU:39, one launch (start us, length us, event | category | flops | bytes accessed | tf_op | source)
XLA Modules:
  0.0 126.8 jit_solution(8403619446834612083)
XLA Ops:
  0.6 0.0 copy-start.1
  0.6 0.0 copy-start
  0.7 0.7 compare_and_fusion
  1.4 1.6 %gather_fusion = bf16[3,2,16,8,32]{4,3,2,1,0:T(8,128)(2,1)S(1)} fusion(bf16[2,6,16,8,32]{4,3,2,1,0:T(8,128)(2,1)} %param.11, s32[1024]{0:T(1024)S(1)} %pad_clamp_fusion), kind=kCustom, calls=%fused_computation | custom fusion | bytes 98316 | tf_op jit(solution)/shard_map/jit(_take)/gather | solution.py:549
  3.0 0.0 copy-start.2
  3.0 0.1 select_bitcast_fusion
  3.1 1.9 %convolution_convert_fusion = bf16[2,3,8,32,128]{4,3,2,1,0:T(8,128)(2,1)} fusion(bf16[2,3,16,8,32]{4,3,2,0,1:T(8,128)(2,1)S(1)} %select_bitcast_fusion, bf16[16,64]{1,0:T(8,128)(2,1)} %bitcast.44), kind=kOutput, calls=%fused_computation.1 | convolution fusion | flops 6496256 | bytes 444416 | tf_op jit(solution)/shard_map/tbcyx,oc->tbyxo/dot_general | solution.py:550
  4.9 0.0 copy-done
  5.0 0.8 pad_maximum_fusion.1.hid_in
  5.8 0.0 copy-done.1
  5.8 0.8 pad_maximum_fusion.2.mem_in
  6.6 0.0 copy-done.2
  6.6 0.9 pad_maximum_fusion.cel_in
  7.5 116.8 %predrnn.1 = (f32[3,8,32,128]{3,2,1,0:T(8,128)}, f32[3,8,32,128]{3,2,1,0:T(8,128)}) custom-call(bf16[6,8,32,128]{3,2,1,0:T(8,128)(2,1)} %bitcast.37, bf16[3,8,32,128]{3,2,1,0:T(8,128)(2,1)} %pad_maximum_fusion.1.hid_in, f32[3,8,32,128]{3,2,1,0:T(8,128)} %pad_maximum_fusion.cel_in, bf16[3,8,32,128]{3,2,1,0:T(8,128)(2,1)} %pad_maximum_fusion.2.mem_in, ...), custom_call_target="tpu_custom_call" | custom-call | tf_op jit(solution)/shard_map/predrnn/pallas_call | solution.py:563
  124.4 2.5 %slice_bitcast_fusion = (f32[1,3,64,8,32]{2,4,3,1,0:T(8,128)}, f32[1,3,64,8,32]{2,4,3,1,0:T(8,128)}, f32[1,3,64,8,32]{2,4,3,1,0:T(8,128)}) fusion(f32[3,8,32,128]{3,2,1,0:T(8,128)} %get-tuple-element.6, f32[3,8,32,128]{3,2,1,0:T(8,128)} %get-tuple-element.5), kind=kLoop, calls=%fused_computation.3 | loop fusion | bytes 1179648 | tf_op jit(solution)/shard_map/broadcast_in_dim | solution.py:631
  (3 shorter events, 0.1 us)
Async XLA Ops:
  0.6 5.2 %copy-start.1 = (f32[3,64,8,32]{1,3,2,0:T(8,128)S(1)}, f32[3,64,8,32]{1,3,2,0:T(8,128)}, u32[]{:S(2)}) copy-start(f32[3,64,8,32]{1,3,2,0:T(8,128)} %param.21) | copy-start | bytes 589828
  0.6 4.3 %copy-start = (f32[1,3,64,8,32]{2,4,3,1,0:T(8,128)S(1)}, f32[1,3,64,8,32]{2,4,3,1,0:T(8,128)}, u32[]{:S(2)}) copy-start(f32[1,3,64,8,32]{2,4,3,1,0:T(8,128)} %param.19) | copy-start | bytes 589828
  3.0 3.6 %copy-start.2 = (f32[1,3,64,8,32]{2,4,3,1,0:T(8,128)S(1)}, f32[1,3,64,8,32]{2,4,3,1,0:T(8,128)}, u32[]{:S(2)}) copy-start(f32[1,3,64,8,32]{2,4,3,1,0:T(8,128)} %param.20) | copy-start | bytes 589828
